TPU v7x, 128 devices: a whole 4x4x4 slice. The times are simulated.
128 devices in a mesh: sec: 2 (over x_lo), batch: 32 (over z, y, core), head: 2 (over x_hi).
Axes of the slice: x: 4 (x_hi: 2, x_lo: 2; x = x_hi * 2 + x_lo), y: 4, z: 4, core: 2. Of those that a mesh axis runs over, the one named last changes fastest.
Arguments:
- hidden_in: bfloat16 [1024, 7168], P('batch'), may hold values from -6 to 6
- queries: bfloat16 [1024, 128, 576], P('batch', ('sec', 'head')), may hold values from -8 to 8
- latent_cache: bfloat16 [1024, 192, 576], P('batch'), may hold values from -8 to 8
- new_latent: bfloat16 [1024, 576], P('batch'), may hold values from -8 to 8
- cache_lengths: int32 [1024], P('batch'), may hold values from 1 to 192, 98304 in all
- value_up: bfloat16 [128, 512, 128], P(('sec', 'head')), may hold values from -0.25 to 0.25
- out_proj: bfloat16 [16384, 7168], P(('sec', 'head'), 'batch'), may hold values from -0.046875 to 0.046875
- norm_gain: float32 [7168], replicated, may hold values from 0.1 to 1.9
- router: bfloat16 [7168, 32], replicated, may hold values from -0.03125 to 0.03125
- expert_ids: int32 [1024, 8], P('batch'), may hold values from 0 to 31, all different within a row; in each aligned block of 32 rows (0 to 31, 32 to 63, ...) at most 16 rows name the same one
- w_gate_up: bfloat16 [32, 7168, 2, 1024], P('batch', None, None, ('sec', 'head')), may hold values from -0.0625 to 0.0625
- w_down: bfloat16 [32, 1024, 7168], P('batch', ('sec', 'head')), may hold values from -0.1875 to 0.1875
Outputs:
- mixed_out: bfloat16 [1024, 7168], P('batch', ('sec', 'head'))
Inputs may be any that keep to these rules, and one draw needn't show every extreme that they name: `expert_ids`: each row names 8 different experts. Among the 32 rows of one index of batch (aligned blocks) no expert is named by more than 16 rows, a bound that some block reaches. `cache_lengths`: the lengths of all rows add up to 98304, and one row has exactly 192.
All inputs are finite; a program needn't handle non-finite values. No bound on the sum of `cache_lengths` on one device may be relied on, other than what follows from the above.
Results may differ from a plain program's by a relative error of at most 0.007.
Values may be sent and summed in bfloat16 or wider, within the bound.
A program may use at most 128 MiB of HBM per device.

v0:
```python
import jax
import jax.numpy as jnp
from jax import lax
from jax.sharding import PartitionSpec as P

QKD = 192
TOP = 8


norm_epsilon = 1e-06
route_scale = 2.5


def body(
    hidden_in,
    queries,
    latent_cache,
    new_latent,
    cache_lengths,
    value_up,
    out_proj,
    norm_gain,
    router,
    expert_ids,
    w_gate_up,
    w_down,
):
    row_count = hidden_in.shape[0]
    model_width = hidden_in.shape[1]
    latent_width = value_up.shape[1]
    cache_depth = latent_cache.shape[1]
    group_count = lax.axis_size("batch")
    slice_count = lax.axis_size(("sec", "head"))
    slice_index = lax.axis_index(("sec", "head"))
    column_width = model_width // slice_count
    capacity = min(row_count, 2 * row_count * TOP // group_count)
    score_scale = QKD ** (-0.5)
    scores = (
        jnp.einsum("thk,tjk->thj", queries, latent_cache, preferred_element_type=jnp.float32)
        * score_scale
    )
    own_score = (
        jnp.einsum("thk,tk->th", queries, new_latent, preferred_element_type=jnp.float32)
        * score_scale
    )
    positions = lax.broadcasted_iota(jnp.int32, (1, 1, cache_depth), 2)
    in_cache = positions < cache_lengths[:, None, None]
    scores = jnp.where(in_cache, scores, -jnp.inf)
    top_score = jnp.maximum(jnp.max(scores, axis=2), own_score)
    cache_exp = jnp.exp(scores - top_score[:, :, None])
    own_exp = jnp.exp(own_score - top_score)
    softmax_sum = jnp.sum(cache_exp, axis=2) + own_exp
    cache_weights = (cache_exp / softmax_sum[:, :, None]).astype(jnp.bfloat16)
    own_weights = (own_exp / softmax_sum).astype(jnp.bfloat16)
    latent_out = jnp.einsum(
        "thj,tjc->thc",
        cache_weights,
        latent_cache[:, :, :latent_width],
        preferred_element_type=jnp.float32,
    )
    latent_out = latent_out + own_weights.astype(jnp.float32)[:, :, None] * new_latent[
        :, None, :latent_width
    ].astype(jnp.float32)
    latent_out = latent_out.astype(jnp.bfloat16)
    head_out = jnp.einsum(
        "thc,hcd->thd", latent_out, value_up, preferred_element_type=jnp.float32
    ).astype(jnp.bfloat16)
    head_out = head_out.reshape(row_count, -1)
    column_part = jnp.dot(
        lax.all_gather(head_out, "batch", axis=0, tiled=True),
        out_proj,
        preferred_element_type=jnp.float32,
    )
    row_part = lax.all_to_all(column_part, "batch", split_axis=0, concat_axis=1, tiled=True)
    attention = lax.psum(row_part, ("sec", "head"))
    residual = hidden_in.astype(jnp.float32) + attention
    mean_square = jnp.mean(residual * residual, axis=1, keepdims=True)
    normed = (residual * lax.rsqrt(mean_square + norm_epsilon) * norm_gain).astype(jnp.bfloat16)
    logits = jnp.dot(normed, router, preferred_element_type=jnp.float32)
    affinity = jax.nn.sigmoid(logits)
    expert_grid = lax.broadcasted_iota(jnp.int32, (1, 1, group_count), 2)
    hit_table = expert_ids[:, :, None] == expert_grid
    picked = jnp.sum(jnp.where(hit_table, affinity[:, None, :], 0.0), axis=2)
    route_weights = route_scale * picked / jnp.sum(picked, axis=1, keepdims=True)
    flat_hits = hit_table.reshape(row_count * TOP, group_count).astype(jnp.int32)
    earlier = jnp.cumsum(flat_hits, axis=0) - flat_hits
    slot_index = jnp.sum(earlier * flat_hits, axis=1)
    position = expert_ids.reshape(-1) * capacity + slot_index
    buffer_grid = lax.broadcasted_iota(jnp.int32, (1, group_count * capacity), 1)
    place_table = (position[:, None] == buffer_grid).astype(jnp.bfloat16)
    dispatch_table = jnp.sum(place_table.reshape(row_count, TOP, group_count * capacity), axis=1)
    gate_up_weight = w_gate_up[0].reshape(model_width, -1)
    hidden_share = w_down.shape[1]
    outgoing = jnp.einsum("rs,rd->sd", dispatch_table, normed, preferred_element_type=jnp.float32)
    outgoing = outgoing.astype(jnp.bfloat16).reshape(group_count, capacity, model_width)
    arrived = lax.all_to_all(outgoing, "batch", split_axis=0, concat_axis=0, tiled=True)
    flat_in = arrived.reshape(-1, model_width)
    gate_up = jnp.dot(flat_in, gate_up_weight, preferred_element_type=jnp.float32)
    activated = (jax.nn.silu(gate_up[:, :hidden_share]) * gate_up[:, hidden_share:]).astype(
        jnp.bfloat16
    )
    result = jnp.dot(activated, w_down[0], preferred_element_type=jnp.float32)
    partial_out = result.reshape(arrived.shape[0], arrived.shape[1], model_width)
    summed_out = lax.psum_scatter(partial_out, ("sec", "head"), scatter_dimension=2, tiled=True)
    returned = lax.all_to_all(summed_out, "batch", split_axis=0, concat_axis=0, tiled=True)
    flat_back = returned.reshape(group_count * capacity, column_width)
    gathered = flat_back[position].reshape(row_count, TOP, column_width)
    mixture = jnp.sum(gathered * route_weights[:, :, None], axis=1)
    residual_cols = lax.dynamic_slice_in_dim(residual, slice_index * column_width, column_width, 1)
    return (residual_cols + mixture).astype(jnp.bfloat16)


def solution(mesh):
    in_specs = (
        P("batch", None),
        P("batch", ("sec", "head"), None),
        P("batch", None, None),
        P("batch", None),
        P("batch"),
        P(("sec", "head"), None, None),
        P(("sec", "head"), "batch"),
        P(),
        P(),
        P("batch", None),
        P("batch", None, None, ("sec", "head")),
        P("batch", ("sec", "head"), None),
    )
    out_specs = P("batch", ("sec", "head"))
    return jax.shard_map(body, mesh=mesh, in_specs=in_specs, out_specs=out_specs, check_vma=False)
```

profile of v0, /device:TPU:0, one launch (start us, length us, event | category | flops | bytes accessed | tf_op | source)
XLA Modules:
  0.0 588.6 jit_solution(7912476928784417901)
XLA Ops:
  6.5 0.0 copy-start
  6.5 0.0 all-gather.2.cloned.1.call-start
  6.5 0.9 iota_compare_fusion.4
  7.4 0.8 slice_convert_fusion
  8.2 1.8 fusion.19
  10.0 0.0 copy-start.2
  10.0 6.8 %fusion.28 = (f32[32,32]{1,0:T(8,128)S(1)}, f32[32,32,192]{2,1,0:T(8,128)S(1)}) fusion(bf16[32,32,576]{2,1,0:T(8,128)(2,1)} %param.13, bf16[32,192,576]{2,1,0:T(8,128)(2,1)} %param.14, pred[32,192]{1,0:T(8,128)(4,1)S(1)} %iota_compare_fusion.4), kind=kOutput, calls=%fused_computation.60 | convolution fusion | flops 227081216 | bytes 9054208 | tf_op jit(solution)/shard_map/thk,tjk->thj/dot_general | solution.py:39
  16.8 0.4 fusion.13
  17.2 0.0 copy-done.2
  17.2 0.0 copy-start.3
  17.2 1.5 add_convert_fusion
  18.8 0.6 copy-done.3
  19.4 1.1 fusion.8
  20.5 0.8 copy.55
  21.2 0.0 all-gather.2.cloned.1.call-update
  21.2 0.0 all-reduce.2.cloned.1.call-start
  21.3 55.6 %all-gather.2.cloned.1.call-done = bf16[1024,4096]{1,0:T(8,128)(2,1)} async-done(((bf16[32,4096]{1,0:T(8,128)(2,1)}), bf16[1024,4096]{1,0:T(8,128)(2,1)}) %all-gather.2.cloned.1.call-update) | async-done | bytes 8388624 | tf_op jit(solution)/shard_map/all_gather | solution.py:70
  76.9 0.0 copy-done
  76.9 5.7 fusion.29
  82.6 0.0 copy-start.8
  82.6 0.0 copy-start.5
  82.7 22.8 %all_to_all.29 = f32[32,32,224]{2,1,0:T(8,128)S(1)} all-to-all(f32[32,32,224]{2,1,0:T(8,128)S(1)} %bitcast.63), channel_id=1, replica_groups=mesh['sec'=2,'batch'=32,'head'=2] {'batch'}, dimensions={0} | all-to-all | bytes 1835008 | tf_op jit(solution)/shard_map/all_to_all | solution.py:74
  105.4 0.0 copy-start.7
  105.4 0.6 copy.37
  106.0 1.6 all_to_all.23
  107.6 0.0 all-reduce.2.cloned.1.call-update
  107.6 0.0 copy-done.8
  107.7 0.1 copy.38
  107.7 0.1 eq.50
  107.8 0.1 eq.46
  107.9 0.6 reduce-window.6
  108.5 0.2 slice_reduce_fusion
  108.8 0.1 fusion.23
  108.9 0.1 reduce_sum.72
  109.0 0.2 fusion.18
  109.2 41.3 %all-reduce.2.cloned.1.call-done = f32[32,7168]{1,0:T(8,128)} async-done(((f32[32,7168]{1,0:T(8,128)}), f32[32,7168]{1,0:T(8,128)}) %all-reduce.2.cloned.1.call-update) | async-done | bytes 917520 | tf_op jit(solution)/shard_map/psum | solution.py:75
  150.5 0.0 copy-done.5
  150.5 1.4 multiply_reduce_fusion
  151.9 0.0 copy-done.7
  151.9 5.1 convolution_convert_fusion
  157.1 7.4 %all-to-all-start.1 = ((bf16[32,16,7168]{2,1,0:T(8,128)(2,1)}), bf16[32,16,7168]{2,1,0:T(8,128)(2,1)}, u32[]{:S(2)}, u32[]{:S(2)}) async-start(bf16[32,16,7168]{2,1,0:T(8,128)(2,1)} %bitcast.58), calls=%async_computation.1 | async-start | bytes 14680064 | tf_op jit(solution)/shard_map/all_to_all | solution.py:96
  164.5 0.2 reduce-scatter.2.cloned.1.call-start
  164.7 7.3 %copy.48 = bf16[896,8,2,256]{3,1,2,0:T(8,128)(2,1)} copy(bf16[896,8,2,256]{3,2,1,0:T(2,128)(2,1)} %bitcast.59) | data formatting | bytes 14680064
  172.0 84.8 %all-to-all-done.1 = bf16[32,16,7168]{2,1,0:T(8,128)(2,1)} async-done(((bf16[32,16,7168]{2,1,0:T(8,128)(2,1)}), bf16[32,16,7168]{2,1,0:T(8,128)(2,1)}, u32[]{:S(2)}, u32[]{:S(2)}) %all-to-all-start.1) | async-done | bytes 7340064 | tf_op jit(solution)/shard_map/all_to_all | solution.py:96
  256.8 0.0 copy-start.4
  256.8 8.6 %fusion.30 = f32[512,512]{1,0:T(8,128)S(1)} fusion(bf16[512,7168]{1,0:T(8,128)(2,1)} %bitcast.8, bf16[7168,512]{1,0:T(8,128)(2,1)} %bitcast.60), kind=kOutput, calls=%fused_computation.62 | convolution fusion | flops 3758096384 | bytes 15728640 | tf_op jit(solution)/shard_map/dot_general | solution.py:98
  265.3 0.2 fusion.14
  265.5 0.0 copy-done.4
  265.5 7.3 %fusion.2 = f32[32,16,7168]{2,1,0:T(8,128)} fusion(bf16[32,16,256]{2,1,0:T(8,128)(2,1)S(1)} %bitcast.62, bf16[1,256,7168]{2,1,0:T(8,128)(2,1)S(1)} %copy-done.4), kind=kOutput, calls=%fused_computation.4 | convolution fusion | flops 1879048192 | bytes 18612224 | tf_op jit(solution)/shard_map/dot_general | solution.py:102
  272.8 0.0 reduce-scatter.2.cloned.1.call-update
  272.8 0.0 copy-start.6
  272.9 245.9 %reduce-scatter.2.cloned.1.call-done = f32[32,16,1792]{2,1,0:T(8,128)} async-done(((f32[32,16,7168]{2,1,0:T(8,128)}), f32[32,16,1792]{2,1,0:T(8,128)}) %reduce-scatter.2.cloned.1.call-update) | async-done | bytes 3670032 | tf_op jit(solution)/shard_map/reduce_scatter | solution.py:104
  518.7 7.4 %all-to-all-start.2 = ((f32[32,16,1792]{2,1,0:T(8,128)}), f32[32,16,1792]{2,1,0:T(8,128)}, u32[]{:S(2)}, u32[]{:S(2)}) async-start(f32[32,16,1792]{2,1,0:T(8,128)} %reduce-scatter.2.cloned.1.call-done), calls=%async_computation.3 | async-start | bytes 7340032 | tf_op jit(solution)/shard_map/all_to_all | solution.py:105
  526.1 0.1 mul.116
  526.2 0.0 copy-done.6
  526.3 0.3 fusion.11
  526.6 0.5 select_reduce_fusion
  527.1 0.1 multiply_divide_fusion
  527.2 46.6 %all-to-all-done.2 = f32[32,16,1792]{2,1,0:T(8,128)} async-done(((f32[32,16,1792]{2,1,0:T(8,128)}), f32[32,16,1792]{2,1,0:T(8,128)}, u32[]{:S(2)}, u32[]{:S(2)}) %all-to-all-start.2) | async-done | bytes 3670048 | tf_op jit(solution)/shard_map/all_to_all | solution.py:105
  573.8 0.0 copy-start.1
  573.8 5.5 gather_fusion
  579.3 2.1 fusion.4
  581.4 0.7 add_convert_fusion.1
  582.1 0.0 copy-done.1
  (9 shorter events, 0.1 us)
Async XLA Ops:
  6.5 70.3 %copy-start = (bf16[4096,224]{0,1:T(8,128)(2,1)S(1)}, bf16[4096,224]{0,1:T(8,128)(2,1)}, u32[]{:S(2)}) copy-start(bf16[4096,224]{0,1:T(8,128)(2,1)} %param.18) | copy-start | bytes 5505028
  6.5 70.3 %all-gather.2.cloned.1.call-start = ((), (), s32[]{:S(2)}) async-start(), calls=%async_computation.4 | async-start | bytes 8650752 | tf_op jit(solution)/shard_map/all_gather | solution.py:70
  10.0 7.2 %copy-start.2 = (bf16[32,192,576]{2,1,0:T(8,128)(2,1)S(1)}, bf16[32,192,576]{2,1,0:T(8,128)(2,1)}, u32[]{:S(2)}) copy-start(bf16[32,192,576]{2,1,0:T(8,128)(2,1)} %param.14) | copy-start | bytes 21233668
  17.2 2.2 copy-start.3
  21.2 129.3 %all-reduce.2.cloned.1.call-start = ((), (), s32[]{:S(2)}) async-start(), calls=%async_computation.5 | async-start | bytes 1835008 | tf_op jit(solution)/shard_map/psum | solution.py:75
  82.6 25.0 %copy-start.8 = (s32[32,8]{0,1:T(8,128)S(1)}, s32[32,8]{0,1:T(8,128)}, u32[]{:S(2)}) copy-start(s32[32,8]{0,1:T(8,128)} %param.21) | copy-start | bytes 3076
  82.6 67.9 %copy-start.5 = (bf16[32,7168]{1,0:T(8,128)(2,1)S(1)}, bf16[32,7168]{1,0:T(8,128)(2,1)}, u32[]{:S(2)}) copy-start(bf16[32,7168]{1,0:T(8,128)(2,1)} %param.12) | copy-start | bytes 1376260
  105.4 46.5 %copy-start.7 = (f32[7168]{0:T(1024)S(1)}, f32[7168]{0:T(1024)}, u32[]{:S(2)}) copy-start(f32[7168]{0:T(1024)} %param.19) | copy-start | bytes 86020
  157.1 99.7 %all-to-all-start.1 = ((bf16[32,16,7168]{2,1,0:T(8,128)(2,1)}), bf16[32,16,7168]{2,1,0:T(8,128)(2,1)}, u32[]{:S(2)}, u32[]{:S(2)}) async-start(bf16[32,16,7168]{2,1,0:T(8,128)(2,1)} %bitcast.58), calls=%async_computation.1 | async-start | bytes 14680064 | tf_op jit(solution)/shard_map/all_to_all | solution.py:96
  164.5 354.3 %reduce-scatter.2.cloned.1.call-start = ((), (), s32[]{:S(2)}) async-start(), calls=%async_computation.6 | async-start | bytes 18350080 | tf_op jit(solution)/shard_map/reduce_scatter | solution.py:104
  256.8 8.8 %copy-start.4 = (bf16[1,256,7168]{2,1,0:T(8,128)(2,1)S(1)}, bf16[1,256,7168]{2,1,0:T(8,128)(2,1)}, u32[]{:S(2)}) copy-start(bf16[1,256,7168]{2,1,0:T(8,128)(2,1)} %param.23) | copy-start | bytes 11010052
  272.8 253.4 %copy-start.6 = (bf16[7168,32]{0,1:T(8,128)(2,1)S(1)}, bf16[7168,32]{0,1:T(8,128)(2,1)}, u32[]{:S(2)}) copy-start(bf16[7168,32]{0,1:T(8,128)(2,1)} %param.20) | copy-start | bytes 1376260
  518.7 55.1 %all-to-all-start.2 = ((f32[32,16,1792]{2,1,0:T(8,128)}), f32[32,16,1792]{2,1,0:T(8,128)}, u32[]{:S(2)}, u32[]{:S(2)}) async-start(f32[32,16,1792]{2,1,0:T(8,128)} %reduce-scatter.2.cloned.1.call-done), calls=%async_computation.3 | async-start | bytes 7340032 | tf_op jit(solution)/shard_map/all_to_all | solution.py:105
  573.8 8.3 %copy-start.1 = (bf16[4096,224]{0,1:T(8,128)(2,1)S(1)}, bf16[4096,224]{0,1:T(8,128)(2,1)}, u32[]{:S(2)}) copy-start(bf16[4096,224]{0,1:T(8,128)(2,1)} %param.18) | copy-start | bytes 5505028
Sparse Core Ops, SparseCore 0:
  21.4 55.4 all-gather.1
  107.8 42.6 all-reduce.1
  273.0 245.7 reduce-scatter.1
where the time goes:
time: 589 us
  waiting for transfers between devices  474 us (80%)
  matrix products  38.3 us (7%)
  blocking collectives  22.8 us (4%)
  local copies, waits for them, and re-layouts  17.1 us (3%)
  starting transfers between devices  15 us (3%)
  between operations  13.3 us (2%)
  other arithmetic  7.99 us (1%)
    reduce_scatter x1, waiting for transfers between devices, body(): lax.psum_scatter(partial_out, ('sec', 'head'), scatter_dimension=2, tiled...  246 us
    all_to_all x1, waiting for transfers between devices, body(): lax.all_to_all(outgoing, 'batch', split_axis=0, concat_axis=0, tiled=True)  84.8 us
    all_gather x1, waiting for transfers between devices, body(): lax.all_gather(head_out, 'batch', axis=0, tiled=True)  55.6 us
    all_to_all x1, waiting for transfers between devices, body(): lax.all_to_all(summed_out, 'batch', split_axis=0, concat_axis=0, tiled=True)  46.6 us
    psum x1, waiting for transfers between devices, body(): attention = lax.psum(row_part, ('sec', 'head'))  41.3 us
    all_to_all x1, blocking collectives, body(): lax.all_to_all(column_part, 'batch', split_axis=0, concat_axis=1, tiled=T...  22.8 us
  transfers between devices with their start and end apart: 5, of which 5 were waited for; matrix products, arithmetic and copies ran while one was open for 2% of the time, Pallas kernels for 0%

commit v1 on v0

v1 whole, which is shorter than its diff:
```python
import jax
import jax.numpy as jnp
from jax import lax
from jax.experimental import pallas as pl
from jax.experimental.pallas import tpu as pltpu
from jax.sharding import PartitionSpec as P

QKD = 192
TOP = 8
norm_epsilon = 1e-06
route_scale = 2.5

BF16, F32 = jnp.bfloat16, jnp.float32
MESH = pl.DeviceIdType.MESH
PARTS = ((0, 640, 1280), (1280, 1920, 2560), (2560, 3200, 3712))
HALF = 3584


def dot(a, b):
    return lax.dot_general(a, b, (((1,), (0,)), ((), ())), preferred_element_type=F32)


def dot_t(a, b):
    return lax.dot_general(a, b, (((1,), (1,)), ((), ())), preferred_element_type=F32)


def layer_kernel(
    head_hbm, wo_hbm, wgu_hbm, wd_hbm, hid_ref, gain_ref, router_ref, ids_ref,
    out_ref,
    H, WO, ACC, PS, RX, SS, RY, MS, MR, RF, RL, X, WGU, GU, WD, A, Y0, Y1, OWN, R0, R1, T0, T1, Q0, Q1,
    ring_s, ring_r, bx_s, bx_r, by_s, by_r, m_s, m_r, rl_s, rl_r, wo_s, wo_r, wg_s, wg_r, wd_s, wd_r, wf_s, wf_r,
    y1_s, y1_r, y2_s, y2_r, loc,
):
    sec = lax.axis_index("sec")
    head = lax.axis_index("head")
    batch = lax.axis_index("batch")
    core = batch % 2
    y = (batch // 2) % 4
    z = batch // 8
    x = head * 2 + sec
    p = z * 4 + y

    def at(zz=None, yy=None, cc=None, xx=None):
        zz = z if zz is None else zz
        yy = y if yy is None else yy
        cc = core if cc is None else cc
        xx = x if xx is None else xx
        return (xx % 2, zz * 8 + yy * 2 + cc, xx // 2)

    def rcopy(src, dst, send, recv, to):
        return pltpu.make_async_remote_copy(
            src_ref=src, dst_ref=dst, send_sem=send, recv_sem=recv, device_id=to, device_id_type=MESH
        )

    def lcopy(src, dst, k):
        return pltpu.make_async_copy(src, dst, loc.at[k])

    sends = []

    def go(copy):
        copy.start()
        sends.append(copy)
        return copy

    own_head = lcopy(head_hbm, H.at[z, y], 0)
    own_head.start()
    own_wo = lcopy(wo_hbm, WO.at[core], 1)
    own_wo.start()

    def own_wgu_step(i, carry):
        for h in range(2):
            lcopy(wgu_hbm.at[i, h], WGU.at[core, h, pl.ds(pl.multiple_of(i * 224, 16), 224)], 2).start()
        return carry

    lax.fori_loop(0, 16, own_wgu_step, 0)

    def wd_cols(xx):
        s = (xx % 2) * 2 + xx // 2
        return wd_hbm.at[:, pl.ds(pl.multiple_of(s * 1792, 128), 1792)]

    own_wd = lcopy(wd_cols(x), WD.at[x, core], 3)
    own_wd.start()

    barrier = pltpu.get_barrier_semaphore()

    def greet(to):
        pl.semaphore_signal(barrier, inc=1, device_id=to, device_id_type=MESH)

    greet(at(cc=1 - core))
    for d in range(1, 4):
        greet(at(xx=(x + d) % 4))
    for d in range(1, 16):
        q = (p + d) % 16
        greet(at(zz=q // 4, yy=q % 4))
    pl.semaphore_wait(barrier, 19)

    dims = {"z": z, "y": y, "x": x}

    def neighbour(dim, d):
        i = (dims[dim] + d) % 4
        return at(zz=i) if dim == "z" else at(yy=i) if dim == "y" else at(xx=i)

    class Ring:
        def __init__(self, k, dim, full, low, high):
            self.k, self.dim, self.full, self.low, self.high = k, dim, full, low, high

        def copy(self, part, i, d, j):
            i = (dims[self.dim] + i) % 4
            return rcopy(part(i), part(i), ring_s.at[self.k, j], ring_r.at[self.k, j], neighbour(self.dim, d))

        def start(self):
            self.up = go(self.copy(self.full, 0, 1, 0))
            self.down = go(self.copy(self.full, 0, 3, 1))

        def forward(self):
            self.up.wait_recv()
            self.far_up = go(self.copy(self.low, 3, 1, 2))
            self.down.wait_recv()
            self.far_down = go(self.copy(self.high, 1, 3, 3))

        def finish(self):
            self.far_up.wait_recv()
            self.far_down.wait_recv()

    def head_ring(k, dim, half, other_full):
        def view(rows):
            def part(i):
                cols = pl.ds(half * 2048, 2048)
                if dim == "z":
                    return H.at[i, :, rows, cols] if other_full else H.at[i, y, rows, cols]
                return H.at[:, i, rows, cols] if other_full else H.at[z, i, rows, cols]

            return part

        return Ring(k, dim, view(pl.ds(0, 32)), view(pl.ds(0, 16)), view(pl.ds(16, 16)))

    h0a, h0b = head_ring(0, "y", 0, False), head_ring(1, "z", 0, True)
    h1a, h1b = head_ring(2, "z", 1, False), head_ring(3, "y", 1, True)

    own_head.wait()
    h0a.start()
    h1a.start()
    other_core = at(cc=1 - core)
    send_wo = go(rcopy(wo_hbm, WO.at[core], wo_s.at[0], wo_r.at[0], other_core))
    send_wd = []
    for d in (1, 3, 2):
        xx = (x + d) % 4
        send_wd.append(go(rcopy(wd_cols(xx), WD.at[x, core], wd_s.at[d - 1], wd_r.at[d - 1], at(xx=xx))))

    def far_wgu(i, h):
        return rcopy(
            wgu_hbm.at[i, h], WGU.at[core, h, pl.ds(pl.multiple_of(i * 224, 16), 224)], wg_s.at[0], wg_r.at[0], other_core
        )

    def far_wgu_step(i, carry):
        for h in range(2):
            far_wgu(i, h).start()
        return carry

    lax.fori_loop(0, 16, far_wgu_step, 0)
    wgu_all = rcopy(WGU.at[core], WGU.at[core], wg_s.at[0], wg_r.at[0], other_core)

    ACC[...] = jnp.zeros_like(ACC)
    h0a.forward()
    h1a.forward()
    h0a.finish()
    h0b.start()
    h1a.finish()
    h1b.start()

    own_wo.wait()
    send_wo.wait_recv()

    def project_z(zz):
        rows = H[zz, :, :, 0:2048].reshape(128, 2048)
        for n in range(2):
            ACC[n, zz] += dot_t(rows, WO[n, :, 0:2048]).reshape(4, 32, 224)

    def project_y(yy):
        rows = H[:, yy, :, 2048:4096].reshape(128, 2048)
        for n in range(2):
            ACC[n, :, yy] += dot_t(rows, WO[n, :, 2048:4096]).reshape(4, 32, 224)

    def project(d):
        project_z((z + d) % 4)
        project_y((y + d) % 4)

    project(0)
    h0b.forward()
    h1b.forward()
    project(1)
    project(3)
    h0b.finish()
    h1b.finish()
    project(2)

    for r in range(2):
        for h in range(2):
            PS[r * 2 + h] = ACC[h, :, :, r * 16 : r * 16 + 16, :].astype(BF16)
    cross = []
    for d in (2, 1, 3):
        xx = (x + d) % 4
        cross.append(go(rcopy(PS.at[xx], RX.at[x], bx_s.at[d - 1], bx_r.at[d - 1], at(xx=xx))))
    for c in cross:
        c.wait_recv()
    total = PS[x].astype(F32)
    for d in range(1, 4):
        total += RX[(x + d) % 4].astype(F32)
    SS[...] = total.astype(BF16)
    plane = []
    for d in range(1, 16):
        q = (p + d) % 16
        plane.append(go(rcopy(SS.at[q // 4, q % 4], RY.at[p], by_s.at[d - 1], by_r.at[d - 1], at(zz=q // 4, yy=q % 4))))
    RY[p] = SS[z, y]
    for c in plane:
        c.wait_recv()

    RF[...] = RY[...].astype(F32) + hid_ref[...].astype(F32)
    res = jnp.concatenate([RF[i] for i in range(16)], axis=1)
    scaled = res * gain_ref[...]
    lane = lax.broadcasted_iota(jnp.int32, (16, 128), 1)
    square = jnp.sum(res * res, axis=1, keepdims=True)
    note = dot(scaled.astype(BF16), router_ref[...])
    MS[...] = jnp.where(lane == 32, square, note)
    msg = go(rcopy(MS, MR, m_s.at[0], m_r.at[0], at(xx=x + 1 - 2 * sec)))
    to_out = []
    for d in range(1, 4):
        xx = (x + d) % 4
        s = (xx % 2) * 2 + xx // 2
        to_out.append(go(rcopy(RF.at[pl.ds(s * 4, 4)], RL.at[x], rl_s.at[d - 1], rl_r.at[d - 1], at(xx=xx))))
    RL[x] = RF[pl.ds((sec * 2 + head) * 4, 4)]
    msg.wait_recv()
    both = MS[...] + MR[...]
    mean_square = jnp.sum(jnp.where(lane == 32, both, 0.0), axis=1, keepdims=True) / (2 * HALF)
    inv = lax.rsqrt(mean_square + norm_epsilon)
    X[z, y, head, sec, :, 0:HALF] = (scaled * inv).astype(BF16)
    affinity = jax.nn.sigmoid(both * inv)
    expert = lane % 64
    hit = jnp.zeros((16, 128), F32)
    for k in range(TOP):
        hit += jnp.where((ids_ref[:, k : k + 1] == expert) & (expert < 32), 1.0, 0.0)
    picked = jnp.where(hit > 0.0, affinity, 0.0)
    gate = route_scale * picked / jnp.sum(jnp.where(lane < 64, picked, 0.0), axis=1, keepdims=True)
    top = gate.astype(BF16).astype(F32)
    X[z, y, head, sec, :, HALF:] = jnp.where(lane < 64, top, gate - top).astype(BF16)

    def row_ring(k, part, dim, done):
        c0, c1, c2 = PARTS[part]

        def view(a, b):
            def block(i):
                zi = i if dim == "z" else slice(None) if "z" in done else z
                yi = i if dim == "y" else slice(None) if "y" in done else y
                if "x" in done:
                    return X.at[zi, yi, :, :, :, pl.ds(a, b - a)]
                xi = i if dim == "x" else x
                return X.at[zi, yi, xi // 2, xi % 2, :, pl.ds(a, b - a)]

            return block

        return Ring(k, dim, view(c0, c2), view(c0, c1), view(c1, c2))

    orders = ("xyz", "yzx", "zxy")
    stages = [
        [row_ring(4 + st * 3 + part, part, orders[part][st], orders[part][:st]) for part in range(3)] for st in range(3)
    ]
    GU[...] = jnp.zeros_like(GU)
    for st in range(3):
        if st > 0:
            for ring, before in zip(stages[st], stages[st - 1]):
                before.finish()
                ring.start()
        else:
            for ring in stages[st]:
                ring.start()
        if st < 2:
            for ring in stages[st]:
                ring.forward()

    for c in send_wd:
        c.wait_recv()
    own_wd.wait()

    pass_on = []
    for i in range(4):
        pass_on.append(go(rcopy(WD.at[i, core], WD.at[i, core], wf_s.at[i], wf_r.at[i], other_core)))
    pltpu.make_async_copy(WGU.at[core], WGU.at[core], loc.at[2]).wait()
    wgu_all.wait_recv()

    def cols(part):
        return PARTS[part][0], min(PARTS[part][2], HALF)

    def experts_z(zz):
        a, b = cols(0)
        for h in range(2):
            rows = X[zz, :, :, h, :, a:b].reshape(128, b - a)
            for e in range(2):
                GU[e, zz] += dot(rows, WGU[e, h, a:b]).reshape(4, 2, 16, 512)

    def experts_x(xx):
        a, b = cols(1)
        r, h = xx // 2, xx % 2
        rows = X[:, :, r, h, :, a:b].reshape(256, b - a)
        for e in range(2):
            GU[e, :, :, r] += dot(rows, WGU[e, h, a:b]).reshape(4, 4, 16, 512)

    def experts_y(yy):
        a, b = cols(2)
        for h in range(2):
            rows = X[:, yy, :, h, :, a:b].reshape(128, b - a)
            for e in range(2):
                GU[e, :, yy] += dot(rows, WGU[e, h, a:b]).reshape(4, 2, 16, 512)

    def experts(d):
        experts_z((z + d) % 4)
        experts_x((x + d) % 4)
        experts_y((y + d) % 4)

    experts(0)
    for ring in stages[2]:
        ring.forward()
    experts(1)
    experts(3)
    for ring in stages[2]:
        ring.finish()
    experts(2)

    def activate(zz, carry):
        gates = X[zz, :, :, 0, :, HALF:].reshape(128, 128).astype(F32)
        wide = lax.broadcasted_iota(jnp.int32, (128, 128), 1) % 64
        for e in range(2):
            weight = jnp.sum(jnp.where(wide == p * 2 + e, gates, 0.0), axis=1, keepdims=True)
            gu = GU[e, zz].reshape(128, 512)
            act = jax.nn.silu(gu[:, :256]) * gu[:, 256:] * weight
            A[x, zz, :, :, e * 256 : e * 256 + 256] = act.astype(BF16).reshape(4, 32, 256)
        return carry

    lax.fori_loop(0, 4, activate, 0)

    act_ring = Ring(13, "x", lambda i: A.at[i], lambda i: A.at[i, pl.ds(0, 2)], lambda i: A.at[i, pl.ds(2, 2)])
    act_ring.start()
    act_ring.forward()
    for c in pass_on:
        c.wait_recv()
    act_ring.finish()

    def down_y(yy):
        acc = jnp.zeros((128, 896), F32)
        for i in range(4):
            acc += dot(A[i, :, yy].reshape(128, 512), WD[i, :, :, 0:896].reshape(512, 896))
        return acc.reshape(4, 32, 896)

    def down_z(zz):
        acc = jnp.zeros((128, 896), F32)
        for i in range(4):
            acc += dot(A[i, zz].reshape(128, 512), WD[i, :, :, 896:1792].reshape(512, 896))
        return acc.reshape(4, 32, 896)

    first = []
    for j, d in enumerate((2, 1, 3)):
        yy, zz = (y + d) % 4, (z + d) % 4
        Y0[j] = down_y(yy).astype(BF16)
        first.append(go(rcopy(Y0.at[j], R0.at[j], y1_s.at[0, j], y1_r.at[0, j], at(yy=yy))))
        Y1[j] = down_z(zz).astype(BF16)
        first.append(go(rcopy(Y1.at[j], R1.at[j], y1_s.at[1, j], y1_r.at[1, j], at(zz=zz))))
    OWN[0] = down_y(y)
    OWN[1] = down_z(z)
    for c in first:
        c.wait_recv()
    for i in range(4):
        t0 = OWN[0, i]
        t1 = OWN[1, i]
        for j in range(3):
            t0 += R0[j, i].astype(F32)
            t1 += R1[j, i].astype(F32)
        OWN[0, i] = t0
        OWN[1, i] = t1
        T0[i] = t0.astype(BF16)
        T1[i] = t1.astype(BF16)
    second = []
    for j, d in enumerate((2, 1, 3)):
        yy, zz = (y + d) % 4, (z + d) % 4
        second.append(go(rcopy(T0.at[zz], Q0.at[j], y2_s.at[0, j], y2_r.at[0, j], at(zz=zz))))
        second.append(go(rcopy(T1.at[yy], Q1.at[j], y2_s.at[1, j], y2_r.at[1, j], at(yy=yy))))
    for c in to_out:
        c.wait_recv()
    for c in second:
        c.wait_recv()
    m0 = OWN[0, z]
    m1 = OWN[1, y]
    for j in range(3):
        m0 += Q0[j].astype(F32)
        m1 += Q1[j].astype(F32)
    for r in range(2):
        rows = slice(r * 16, r * 16 + 16)
        low = jnp.concatenate([RL[r * 2 + h, i] for i in range(2) for h in range(2)], axis=1)
        high = jnp.concatenate([RL[r * 2 + h, i] for i in range(2, 4) for h in range(2)], axis=1)
        out_ref[rows, 0:896] = (low + m0[rows]).astype(BF16)
        out_ref[rows, 896:1792] = (high + m1[rows]).astype(BF16)

    for c in sends:
        c.wait_send()
    wgu_all.wait_send()


def body(
    hidden_in, queries, latent_cache, new_latent, cache_lengths, value_up, out_proj, norm_gain, router, expert_ids,
    w_gate_up, w_down,
):
    row_count = hidden_in.shape[0]
    model_width = hidden_in.shape[1]
    latent_width = value_up.shape[1]
    cache_depth = latent_cache.shape[1]
    sec = lax.axis_index("sec")
    head = lax.axis_index("head")
    score_scale = QKD ** (-0.5)
    scores = jnp.einsum("thk,tjk->thj", queries, latent_cache, preferred_element_type=F32) * score_scale
    own_score = jnp.einsum("thk,tk->th", queries, new_latent, preferred_element_type=F32) * score_scale
    positions = lax.broadcasted_iota(jnp.int32, (1, 1, cache_depth), 2)
    in_cache = positions < cache_lengths[:, None, None]
    scores = jnp.where(in_cache, scores, -jnp.inf)
    top_score = jnp.maximum(jnp.max(scores, axis=2), own_score)
    cache_exp = jnp.exp(scores - top_score[:, :, None])
    own_exp = jnp.exp(own_score - top_score)
    softmax_sum = jnp.sum(cache_exp, axis=2) + own_exp
    cache_weights = (cache_exp / softmax_sum[:, :, None]).astype(BF16)
    own_weights = (own_exp / softmax_sum).astype(BF16)
    latent_out = jnp.einsum(
        "thj,tjc->thc", cache_weights, latent_cache[:, :, :latent_width], preferred_element_type=F32
    )
    latent_out = latent_out + own_weights.astype(F32)[:, :, None] * new_latent[:, None, :latent_width].astype(F32)
    latent_out = latent_out.astype(BF16)
    head_out = jnp.einsum("thc,hcd->thd", latent_out, value_up, preferred_element_type=F32).astype(BF16)
    head_out = head_out.reshape(row_count, -1)

    hid = lax.dynamic_index_in_dim(hidden_in.reshape(2, 16, 16, 2, 224), head, 0, False)
    hid = lax.dynamic_index_in_dim(hid, sec, 2, False).transpose(1, 0, 2)
    gain = lax.dynamic_index_in_dim(norm_gain.reshape(16, 2, 224), sec, 1, False).reshape(1, HALF)
    rout = lax.dynamic_index_in_dim(router.reshape(16, 2, 224, 32), sec, 1, False).reshape(HALF, 32)
    blank = jnp.zeros((HALF, 32), BF16)
    rout = jnp.concatenate([rout, blank, rout, blank], axis=1)
    ids = lax.dynamic_slice_in_dim(expert_ids, head * 16, 16, 0)
    wgu = w_gate_up[0].reshape(16, 2, 224, 512)

    any_spec = pl.BlockSpec(memory_space=pl.ANY)
    vmem = pl.BlockSpec(memory_space=pltpu.VMEM)
    dma = pltpu.SemaphoreType.DMA
    return pl.pallas_call(
        layer_kernel,
        out_shape=jax.ShapeDtypeStruct((32, 1792), BF16),
        in_specs=[any_spec] * 4 + [vmem] * 4,
        out_specs=vmem,
        scratch_shapes=[
            pltpu.VMEM((4, 4, 32, 4096), BF16),
            pltpu.VMEM((2, 224, 4096), BF16),
            pltpu.VMEM((2, 4, 4, 32, 224), F32),
            pltpu.VMEM((4, 4, 4, 16, 224), BF16),
            pltpu.VMEM((4, 4, 4, 16, 224), BF16),
            pltpu.VMEM((4, 4, 16, 224), BF16),
            pltpu.VMEM((16, 16, 224), BF16),
            pltpu.VMEM((16, 128), F32),
            pltpu.VMEM((16, 128), F32),
            pltpu.VMEM((16, 16, 224), F32),
            pltpu.VMEM((4, 4, 16, 224), F32),
            pltpu.VMEM((4, 4, 2, 2, 16, 3712), BF16),
            pltpu.VMEM((2, 2, HALF, 512), BF16),
            pltpu.VMEM((2, 4, 4, 2, 16, 512), F32),
            pltpu.VMEM((4, 2, 256, 1792), BF16),
            pltpu.VMEM((4, 4, 4, 32, 512), BF16),
            pltpu.VMEM((3, 4, 32, 896), BF16),
            pltpu.VMEM((3, 4, 32, 896), BF16),
            pltpu.VMEM((2, 4, 32, 896), F32),
            pltpu.VMEM((3, 4, 32, 896), BF16),
            pltpu.VMEM((3, 4, 32, 896), BF16),
            pltpu.VMEM((4, 32, 896), BF16),
            pltpu.VMEM((4, 32, 896), BF16),
            pltpu.VMEM((3, 32, 896), BF16),
            pltpu.VMEM((3, 32, 896), BF16),
            dma((14, 4)),
            dma((14, 4)),
            dma((3,)),
            dma((3,)),
            dma((15,)),
            dma((15,)),
            dma((1,)),
            dma((1,)),
            dma((3,)),
            dma((3,)),
            dma((1,)),
            dma((1,)),
            dma((1,)),
            dma((1,)),
            dma((3,)),
            dma((3,)),
            dma((4,)),
            dma((4,)),
            dma((2, 3)),
            dma((2, 3)),
            dma((2, 3)),
            dma((2, 3)),
            dma((4,)),
        ],
        compiler_params=pltpu.CompilerParams(
            collective_id=0, has_side_effects=True, vmem_limit_bytes=66_000_000
        ),
        name="layer",
    )(head_out, out_proj.T, wgu, w_down[0], hid, gain, rout, ids)


def solution(mesh):
    in_specs = (
        P("batch", None),
        P("batch", ("sec", "head"), None),
        P("batch", None, None),
        P("batch", None),
        P("batch"),
        P(("sec", "head"), None, None),
        P(("sec", "head"), "batch"),
        P(),
        P(),
        P("batch", None),
        P("batch", None, None, ("sec", "head")),
        P("batch", ("sec", "head"), None),
    )
    out_specs = P("batch", ("sec", "head"))
    return jax.shard_map(body, mesh=mesh, in_specs=in_specs, out_specs=out_specs, check_vma=False)
```

time: 589 us -> 182 us (0.31)
  waiting for transfers between devices: 474 us -> 0 us
  Pallas kernels: 0 us -> 142 us
  matrix products: 38.3 us -> 13.3 us
  blocking collectives: 22.8 us -> 0 us
  starting transfers between devices: 15 us -> 0 us
  between operations: 13.3 us -> 0.12 us
    reduce_scatter x1 -> x0, waiting for transfers between devices: 246 us -> none  [body(): lax.psum_scatter(partial_out, ('sec', 'head'), scatter_dimension=2, tiled...]
    pallas_call x0 -> x1, Pallas kernels: none -> 142 us  [body(): pl.pallas_call(layer_kernel, out_shape=jax.ShapeDtypeStruct((32, 1792), B...]
    all_to_all x2 -> x0, waiting for transfers between devices: 131 us -> none  [the longest x1 84.8 us: body(): lax.all_to_all(outgoing, 'batch', split_axis=0, concat_axis=0, tiled=True)]
    all_gather x1 -> x0, waiting for transfers between devices: 55.6 us -> none  [body(): lax.all_gather(head_out, 'batch', axis=0, tiled=True)]
    psum x1 -> x0, waiting for transfers between devices: 41.3 us -> none  [body(): attention = lax.psum(row_part, ('sec', 'head'))]
    dot_general x7 -> x2, matrix products: 30 us -> 3.26 us  [the longest x1 1.81 us: body(): jnp.einsum('thk,tk->th', queries, new_latent, preferred_element_type=F32)]
    all_to_all x1 -> x0, blocking collectives: 22.8 us -> none  [body(): lax.all_to_all(column_part, 'batch', split_axis=0, concat_axis=1, tiled=T...]
    all_to_all x2 -> x0, starting transfers between devices: 14.8 us -> none  [the longest x1 7.39 us: body(): lax.all_to_all(summed_out, 'batch', split_axis=0, concat_axis=0, tiled=True)]
  transfers between devices with their start and end apart: 5 -> 0, of which waited for: 5 -> 0; matrix products, arithmetic and copies ran while one was open for 2% -> 0% of each run, Pallas kernels for 0% -> 0%
where the time goes in v1:
time: 182 us; the launch traced here: 181 us
  Pallas kernels  142 us (78%)
  local copies, waits for them, and re-layouts  22.3 us (12%)
  matrix products  13.3 us (7%)
  other arithmetic  3.88 us (2%)
    pallas_call x1, Pallas kernels, body(): pl.pallas_call(layer_kernel, out_shape=jax.ShapeDtypeStruct((32, 1792), B...  142 us
    another operation x1, local copies, waits for them, and re-layouts, body(): wgu = w_gate_up[0].reshape(16, 2, 224, 512)  12.4 us
    dot_general x1, matrix products, body(): jnp.einsum('thk,tjk->thj', queries, latent_cache, preferred_element_type=...  6.24 us
    unnamed x14, local copies, waits for them, and re-layouts  4.65 us
    dot_general x1, matrix products, body(): jnp.einsum('thj,tjc->thc', cache_weights, latent_cache[:, :, :latent_widt...  3.75 us

profile of v1, /device:TPU:0, one launch (start us, length us, event | category | flops | bytes accessed | tf_op | source)
XLA Modules:
  0.0 181.4 jit_solution(12005845420471787313)
XLA Ops:
  0.0 0.0 copy-start
  0.0 0.0 copy-start.4
  0.0 0.0 copy-start.3
  0.0 0.7 copy-done
  0.7 0.1 constant_dynamic-slice_fusion
  0.8 0.7 copy.28.ids_ref
  1.4 0.7 iota_compare_fusion
  2.2 1.8 fusion.11
  4.0 0.9 reshape.50
  4.9 0.1 dynamic-slice_reduce_fusion
  4.9 0.7 reshape.51.gain_ref
  5.6 0.8 slice_convert_fusion
  6.4 0.0 copy-done.3
  6.4 0.8 reshape.49
  7.2 0.3 constant_dynamic-slice_fusion.2
  7.5 0.8 copy.39
  8.3 0.0 copy-done.4
  8.3 0.8 reshape.52
  9.1 0.6 constant_dynamic-slice_fusion.1
  9.8 0.7 copy.27
  10.4 0.0 copy-start.2
  10.4 0.1 broadcast_in_dim.22
  10.6 2.0 %pad_maximum_fusion.router_ref = bf16[3584,128]{1,0:T(8,128)(2,1)} fusion(bf16[3584,32]{1,0:T(8,128)(2,1)S(1)} %broadcast_in_dim.22, bf16[3584,32]{1,0:T(8,128)(2,1)S(1)} %bitcast.24), kind=kLoop, calls=%fused_computation.13 | loop fusion | flops 3670016 | bytes 1376256 | tf_op jit(solution)/shard_map/concatenate | solution.py:441
  12.5 0.0 copy-done.2
  12.5 6.2 %fusion.15 = (f32[32,32]{1,0:T(8,128)S(1)}, f32[32,32,192]{2,1,0:T(8,128)S(1)}) fusion(bf16[32,32,576]{2,1,0:T(8,128)(2,1)S(1)} %copy-done.2, bf16[32,192,576]{2,1,0:T(8,128)(2,1)} %param.14, pred[32,192]{1,0:T(8,128)(4,1)S(1)} %iota_compare_fusion), kind=kOutput, calls=%fused_computation.31 | convolution fusion | flops 227081216 | bytes 9054208 | tf_op jit(solution)/shard_map/thk,tjk->thj/dot_general | solution.py:417
  18.8 0.4 fusion.8
  19.2 0.1 copy.18
  19.3 0.0 copy-start.1
  19.3 3.8 %fusion = f32[32,32,512]{2,1,0:T(8,128)S(1)} fusion(bf16[32,192,576]{2,1,0:T(8,128)(2,1)} %param.14, f32[32,32,192]{2,1,0:T(8,128)S(1)} %get-tuple-element.8, f32[32,32]{1,0:T(8,128)S(1)} %get-tuple-element.6, f32[32,32]{1,0:T(8,128)S(1)} %multiply_maximum_fusion), kind=kOutput, calls=%fused_computation | convolution fusion | flops 201916416 | bytes 9183232 | tf_op jit(solution)/shard_map/thj,tjc->thc/dot_general | solution.py:428
  23.0 0.3 copy-done.1
  23.3 1.4 fusion.4
  24.8 0.8 copy.38
  25.6 12.4 %reshape_squeeze.3.wgu_hbm = bf16[16,2,224,512]{3,2,1,0:T(8,128)(2,1)} reshape(bf16[1,7168,2,256]{3,2,1,0:T(2,128)(2,1)} %param.22) | data formatting | bytes 14680064 | tf_op jit(solution)/shard_map/reshape;squeeze | solution.py:443
  38.0 141.9 %layer.1 = bf16[32,1792]{1,0:T(8,128)(2,1)} custom-call(bf16[32,4096]{1,0:T(8,128)(2,1)} %bitcast.26, bf16[224,4096]{1,0:T(8,128)(2,1)} %bitcast.25, bf16[16,2,224,512]{3,2,1,0:T(8,128)(2,1)} %reshape_squeeze.3.wgu_hbm, bf16[256,7168]{1,0:T(8,128)(2,1)} %bitcast.23, bf16[16,16,224]{2,1,0:T(8,128)(2,1)} %bitcast.27, f32[1,3584]{1,0:T(1,128)} %reshape.51.gain_ref, ...), custom_call_target="tpu_custom_call" | custom-call | tf_op jit(solution)/shard_map/layer/pallas_call | solution.py:448
  179.9 1.6 copy.41
  (2 shorter events, 0.0 us)
Async XLA Ops:
  0.0 0.7 copy-start
  0.0 8.3 %copy-start.4 = (bf16[7168,32]{0,1:T(8,128)(2,1)S(1)}, bf16[7168,32]{0,1:T(8,128)(2,1)}, u32[]{:S(2)}) copy-start(bf16[7168,32]{0,1:T(8,128)(2,1)} %param.20) | copy-start | bytes 1376260
  0.0 6.4 %copy-start.3 = (bf16[32,7168]{1,0:T(8,128)(2,1)S(1)}, bf16[32,7168]{1,0:T(8,128)(2,1)}, u32[]{:S(2)}) copy-start(bf16[32,7168]{1,0:T(8,128)(2,1)} %param.12) | copy-start | bytes 1376260
  10.4 2.1 %copy-start.2 = (bf16[32,32,576]{2,1,0:T(8,128)(2,1)S(1)}, bf16[32,32,576]{2,1,0:T(8,128)(2,1)}, u32[]{:S(2)}) copy-start(bf16[32,32,576]{2,1,0:T(8,128)(2,1)} %param.13) | copy-start | bytes 3538948
  19.3 4.0 %copy-start.1 = (bf16[32,512,128]{2,1,0:T(8,128)(2,1)S(1)}, bf16[32,512,128]{2,1,0:T(8,128)(2,1)}, u32[]{:S(2)}) copy-start(bf16[32,512,128]{2,1,0:T(8,128)(2,1)} %param.17) | copy-start | bytes 12582916

commit v2 on v1

v2 whole, which is shorter than its diff:
```python
import jax
import jax.numpy as jnp
from jax import lax
from jax.experimental import pallas as pl
from jax.experimental.pallas import tpu as pltpu
from jax.sharding import PartitionSpec as P

QKD = 192
TOP = 8
norm_epsilon = 1e-06
route_scale = 2.5

BF16, F32 = jnp.bfloat16, jnp.float32
MESH = pl.DeviceIdType.MESH
PARTS = ((0, 640, 1280), (1280, 1920, 2560), (2560, 3200, 3712))
HALF = 3584
GROUP = 8


def dot(a, b):
    return lax.dot_general(a, b, (((1,), (0,)), ((), ())), preferred_element_type=F32)


def dot_t(a, b):
    return lax.dot_general(a, b, (((1,), (1,)), ((), ())), preferred_element_type=F32)


def layer_kernel(
    q_hbm, cache_hbm, vu_hbm, wo_hbm, wgu_hbm, wd_hbm, new_ref, hidden_ref, gain_ref, router_ref, ids_ref, len_ref,
    out_ref,
    CA, Q, NEW, L, VU, RAW, PERM, HID, GAIN, ROUT, HIT,
    H, WO, ACC, PS, RX, SS, RY, MS, MR, RF, RL, X, WGU, GU, WD, A, Y0, Y1, R0, R1, T0, T1, Q0, Q1, O0,
    ring_s, ring_r, bx_s, bx_r, by_s, by_r, m_s, m_r, rl_s, rl_r, wo_s, wo_r, wg_s, wg_r, wd_s, wd_r, wf_s, wf_r,
    y0_s, y0_r, y1_s, y1_r, y2_s, y2_r, loc, ca_sem, raw_sem,
):
    sec = lax.axis_index("sec")
    head = lax.axis_index("head")
    batch = lax.axis_index("batch")
    core = batch % 2
    y = (batch // 2) % 4
    z = batch // 8
    x = head * 2 + sec
    p = z * 4 + y

    def at(zz=None, yy=None, cc=None, xx=None):
        zz = z if zz is None else zz
        yy = y if yy is None else yy
        cc = core if cc is None else cc
        xx = x if xx is None else xx
        return (xx % 2, zz * 8 + yy * 2 + cc, xx // 2)

    barrier = pltpu.get_barrier_semaphore()

    def greet(to):
        pl.semaphore_signal(barrier, inc=1, device_id=to, device_id_type=MESH)

    greet(at(cc=1 - core))
    for d in range(1, 4):
        greet(at(xx=(x + d) % 4))
    for d in range(1, 16):
        q = (p + d) % 16
        greet(at(zz=q // 4, yy=q % 4))

    def rcopy(src, dst, send, recv, to):
        return pltpu.make_async_remote_copy(
            src_ref=src, dst_ref=dst, send_sem=send, recv_sem=recv, device_id=to, device_id_type=MESH
        )

    def lcopy(src, dst, k):
        return pltpu.make_async_copy(src, dst, loc.at[k])

    sends = []

    def go(copy):
        copy.start()
        sends.append(copy)
        return copy

    def cache_copy(g, slot):
        return pltpu.make_async_copy(
            cache_hbm.at[pl.ds(g * GROUP, GROUP)], CA.at[slot, :, pl.ds(0, 192)], ca_sem.at[slot]
        )

    def raw_copy(i, slot):
        rows = pl.ds(pl.multiple_of(i * 3584, 128), 3584)
        return pltpu.make_async_copy(wgu_hbm.at[rows], RAW.at[slot], raw_sem.at[slot])

    own_q = lcopy(q_hbm, Q, 0)
    own_q.start()
    cache_copy(0, 0).start()
    cache_copy(1, 1).start()
    own_vu = lcopy(vu_hbm, VU, 2)
    own_vu.start()
    own_wo = lcopy(wo_hbm, WO.at[core], 1)
    own_wo.start()
    raw_copy(0, 0).start()
    raw_copy(1, 1).start()

    def wd_cols(xx):
        s = (xx % 2) * 2 + xx // 2
        return wd_hbm.at[:, pl.ds(pl.multiple_of(s * 1792, 128), 1792)]

    own_wd = lcopy(wd_cols(x), WD.at[x, core], 3)
    own_wd.start()
    NEW[...] = new_ref[...].astype(F32)
    own_q.wait()
    pl.semaphore_wait(barrier, 19)

    other_core = at(cc=1 - core)
    send_wo = go(rcopy(wo_hbm, WO.at[core], wo_s.at[0], wo_r.at[0], other_core))
    send_wd = []
    for d in (1, 3, 2):
        xx = (x + d) % 4
        send_wd.append(go(rcopy(wd_cols(xx), WD.at[x, core], wd_s.at[d - 1], wd_r.at[d - 1], at(xx=xx))))

    own_row = lax.broadcasted_iota(jnp.int32, (16, 576), 0) == 0
    column = lax.broadcasted_iota(jnp.int32, (GROUP * 32, 208), 1)

    def attend(g, carry):
        slot = g % 2
        cache_copy(g, slot).wait()
        news = [NEW[pl.ds(g * GROUP + i, 1), :] for i in range(GROUP)]
        for i in range(GROUP):
            CA[slot, i, 192:208, :] = jnp.where(own_row, news[i], 0.0).astype(BF16)
        lengths = jnp.concatenate([jnp.full((32, 1), len_ref[g * GROUP + i], jnp.int32) for i in range(GROUP)], axis=0)
        scores = jnp.concatenate([dot_t(Q[g * GROUP + i], CA[slot, i]) for i in range(GROUP)], axis=0) * (QKD**-0.5)
        scores = jnp.where((column < lengths) | (column == 192), scores, -jnp.inf)
        weights = jnp.exp(scores - jnp.max(scores, axis=1, keepdims=True))
        weights = (weights / jnp.sum(weights, axis=1, keepdims=True)).astype(BF16)
        for i in range(GROUP):
            rows = pl.ds(pl.multiple_of((g * GROUP + i) * 32, 32), 32)
            latent = dot(weights[i * 32 : i * 32 + 32], CA[slot, i, :, 0:512])
            for c in range(4):
                L[c, rows, :] = latent[:, c * 128 : c * 128 + 128]

        @pl.when(g + 2 < 32 // GROUP)
        def _():
            cache_copy(g + 2, slot).start()

        return carry

    lax.fori_loop(0, 32 // GROUP, attend, 0)
    own_vu.wait()

    def head_values(h, carry):
        latent = jnp.concatenate([L[c, pl.ds(h, 32, stride=32), :] for c in range(4)], axis=1).astype(BF16)
        H[z, y, :, pl.ds(pl.multiple_of(h * 128, 128), 128)] = dot(latent, VU[h]).astype(BF16)
        return carry

    dims = {"z": z, "y": y, "x": x}

    def neighbour(dim, d):
        i = (dims[dim] + d) % 4
        return at(zz=i) if dim == "z" else at(yy=i) if dim == "y" else at(xx=i)

    class Ring:
        def __init__(self, k, dim, full, low, high):
            self.k, self.dim, self.full, self.low, self.high = k, dim, full, low, high

        def copy(self, part, i, d, j):
            i = (dims[self.dim] + i) % 4
            return rcopy(part(i), part(i), ring_s.at[self.k, j], ring_r.at[self.k, j], neighbour(self.dim, d))

        def start(self):
            self.up = go(self.copy(self.full, 0, 1, 0))
            self.down = go(self.copy(self.full, 0, 3, 1))

        def forward(self):
            self.up.wait_recv()
            self.far_up = go(self.copy(self.low, 3, 1, 2))
            self.down.wait_recv()
            self.far_down = go(self.copy(self.high, 1, 3, 3))

        def finish(self):
            self.far_up.wait_recv()
            self.far_down.wait_recv()

    def head_ring(k, dim, half, other_full):
        def view(rows):
            def part(i):
                cols = pl.ds(half * 2048, 2048)
                if dim == "z":
                    return H.at[i, :, rows, cols] if other_full else H.at[i, y, rows, cols]
                return H.at[:, i, rows, cols] if other_full else H.at[z, i, rows, cols]

            return part

        return Ring(k, dim, view(pl.ds(0, 32)), view(pl.ds(0, 16)), view(pl.ds(16, 16)))

    h0a, h0b = head_ring(0, "y", 0, False), head_ring(1, "z", 0, True)
    h1a, h1b = head_ring(2, "z", 1, False), head_ring(3, "y", 1, True)

    lax.fori_loop(0, 16, head_values, 0)
    h0a.start()
    lax.fori_loop(16, 32, head_values, 0)
    h1a.start()

    spread_row = lax.broadcasted_iota(jnp.int32, (256, 256), 0)
    spread_col = lax.broadcasted_iota(jnp.int32, (256, 256), 1)
    PERM[...] = jnp.where(spread_col == (spread_row % 64) * 4 + spread_row // 64, 1.0, 0.0).astype(BF16)

    def separate(i, carry):
        slot = i % 2
        raw_copy(i, slot).wait()
        for b in range(0, 14, 2):
            pair = jnp.concatenate([RAW[slot, b * 256 : b * 256 + 256], RAW[slot, b * 256 + 256 : b * 256 + 512]], axis=1)
            moved = dot(PERM[...], pair).astype(BF16)
            for j in range(2):
                for u in range(2):
                    k = (b + j) * 64 + u * 32
                    h, row = (k // 224) % 2, k // 448 * 224 + k % 224
                    row = pl.multiple_of(i * 448 + row, 32)
                    for q in range(4):
                        to = q % 2 * 256 + q // 2 * 128
                        a = q * 64 + u * 32
                        WGU[core, h, pl.ds(row, 32), to : to + 128] = moved[a : a + 32, j * 128 : j * 128 + 128]

        @pl.when(i + 2 < 8)
        def _():
            raw_copy(i + 2, slot).start()

        return carry

    def far_wgu(i, h):
        block = WGU.at[core, h, pl.ds(i * 448, 448)]
        return rcopy(block, block, wg_s.at[0], wg_r.at[0], other_core)

    wgu_all = rcopy(WGU.at[core], WGU.at[core], wg_s.at[0], wg_r.at[0], other_core)

    def pieces(v):
        return [jnp.where(sec == 0, v[:, i * 448 : i * 448 + 224], v[:, i * 448 + 224 : i * 448 + 448]) for i in range(16)]

    def pack_inputs():
        for i, piece in enumerate(pieces(hidden_ref[pl.ds(pl.multiple_of(head * 16, 16), 16), :].astype(F32))):
            HID[i] = piece
        GAIN[...] = jnp.concatenate(pieces(gain_ref[...]), axis=1)
        ROUT[0:32, :] = jnp.concatenate(pieces(router_ref[...].astype(F32)), axis=1).astype(BF16)
        ROUT[32:128, :] = jnp.zeros((96, HALF), BF16)
        expert = lax.broadcasted_iota(jnp.int32, (128, 32), 0)
        hit = jnp.zeros((128, 32), F32)
        for k in range(TOP):
            hit += jnp.where(ids_ref[k : k + 1, :] == expert, 1.0, 0.0)
        mine = lax.broadcasted_iota(jnp.int32, (16, 32), 1) == lax.broadcasted_iota(jnp.int32, (16, 32), 0) + head * 16
        HIT[...] = dot_t(jnp.where(mine, 1.0, 0.0).astype(BF16), hit.astype(BF16))

    ACC[...] = jnp.zeros_like(ACC)
    lax.fori_loop(0, 2, separate, 0)
    h0a.forward()
    h1a.forward()
    lax.fori_loop(2, 4, separate, 0)
    h0a.finish()
    h0b.start()
    h1a.finish()
    h1b.start()
    for i in range(4):
        for h in range(2):
            far_wgu(i, h).start()
    lax.fori_loop(4, 8, separate, 0)
    pack_inputs()
    for i in range(4, 8):
        for h in range(2):
            far_wgu(i, h).start()

    own_wo.wait()
    send_wo.wait_recv()

    def project_z(zz):
        rows = H[zz, :, :, 0:2048].reshape(128, 2048)
        for n in range(2):
            ACC[n, zz] += dot_t(rows, WO[n, :, 0:2048]).reshape(4, 32, 224)

    def project_y(yy):
        rows = H[:, yy, :, 2048:4096].reshape(128, 2048)
        for n in range(2):
            ACC[n, :, yy] += dot_t(rows, WO[n, :, 2048:4096]).reshape(4, 32, 224)

    def project(d):
        project_z((z + d) % 4)
        project_y((y + d) % 4)

    project(0)
    h0b.forward()
    h1b.forward()
    project(1)
    project(3)
    h0b.finish()
    h1b.finish()
    project(2)

    for r in range(2):
        for h in range(2):
            PS[r * 2 + h] = ACC[h, :, :, r * 16 : r * 16 + 16, :].astype(BF16)
    cross = []
    for d in (2, 1, 3):
        xx = (x + d) % 4
        cross.append(go(rcopy(PS.at[xx], RX.at[x], bx_s.at[d - 1], bx_r.at[d - 1], at(xx=xx))))
    for c in cross:
        c.wait_recv()
    total = PS[x].astype(F32)
    for d in range(1, 4):
        total += RX[(x + d) % 4].astype(F32)
    SS[...] = total.astype(BF16)
    plane = []
    for d in range(1, 16):
        q = (p + d) % 16
        plane.append(go(rcopy(SS.at[q // 4, q % 4], RY.at[p], by_s.at[d - 1], by_r.at[d - 1], at(zz=q // 4, yy=q % 4))))
    RY[p] = SS[z, y]
    for c in plane:
        c.wait_recv()

    RF[...] = RY[...].astype(F32) + HID[...]
    res = jnp.concatenate([RF[i] for i in range(16)], axis=1)
    scaled = res * GAIN[...]
    lane = lax.broadcasted_iota(jnp.int32, (16, 128), 1)
    square = jnp.sum(res * res, axis=1, keepdims=True)
    note = dot_t(scaled.astype(BF16), ROUT[...])
    MS[...] = jnp.where(lane == 32, square, note)
    msg = go(rcopy(MS, MR, m_s.at[0], m_r.at[0], at(xx=x + 1 - 2 * sec)))
    to_out = []
    for d in range(1, 4):
        xx = (x + d) % 4
        s = (xx % 2) * 2 + xx // 2
        to_out.append(go(rcopy(RF.at[pl.ds(s * 4, 4)], RL.at[x], rl_s.at[d - 1], rl_r.at[d - 1], at(xx=xx))))
    RL[x] = RF[pl.ds((sec * 2 + head) * 4, 4)]
    msg.wait_recv()
    both = MS[...] + MR[...]
    mean_square = jnp.sum(jnp.where(lane == 32, both, 0.0), axis=1, keepdims=True) / (2 * HALF)
    inv = lax.rsqrt(mean_square + norm_epsilon)
    X[z, y, head, sec, :, 0:HALF] = (scaled * inv).astype(BF16)
    affinity = jax.nn.sigmoid(both * inv)
    picked = jnp.where(HIT[...] > 0.0, affinity, 0.0)
    gate = route_scale * picked / jnp.sum(picked, axis=1, keepdims=True)
    top = gate.astype(BF16).astype(F32)
    X[z, y, head, sec, :, HALF:] = (top + pltpu.roll(gate - top, 64, 1)).astype(BF16)

    def row_ring(k, part, dim, done):
        c0, c1, c2 = PARTS[part]

        def view(a, b):
            def block(i):
                zi = i if dim == "z" else slice(None) if "z" in done else z
                yi = i if dim == "y" else slice(None) if "y" in done else y
                if "x" in done:
                    return X.at[zi, yi, :, :, :, pl.ds(a, b - a)]
                xi = i if dim == "x" else x
                return X.at[zi, yi, xi // 2, xi % 2, :, pl.ds(a, b - a)]

            return block

        return Ring(k, dim, view(c0, c2), view(c0, c1), view(c1, c2))

    orders = ("xyz", "yzx", "zxy")
    stages = [
        [row_ring(4 + st * 3 + part, part, orders[part][st], orders[part][:st]) for part in range(3)] for st in range(3)
    ]
    GU[...] = jnp.zeros_like(GU)
    for st in range(3):
        if st > 0:
            for ring, before in zip(stages[st], stages[st - 1]):
                before.finish()
                ring.start()
        else:
            for ring in stages[st]:
                ring.start()
        if st < 2:
            for ring in stages[st]:
                ring.forward()

    for c in send_wd:
        c.wait_recv()
    own_wd.wait()

    pass_on = []
    for i in range(4):
        pass_on.append(go(rcopy(WD.at[i, core], WD.at[i, core], wf_s.at[i], wf_r.at[i], other_core)))
    wgu_all.wait_recv()

    def cols(part):
        return PARTS[part][0], min(PARTS[part][2], HALF)

    def experts_z(zz):
        a, b = cols(0)
        for h in range(2):
            rows = X[zz, :, :, h, :, a:b].reshape(128, b - a)
            for e in range(2):
                GU[e, zz] += dot(rows, WGU[e, h, a:b]).reshape(4, 2, 16, 512)

    def experts_x(xx):
        a, b = cols(1)
        r, h = xx // 2, xx % 2
        rows = X[:, :, r, h, :, a:b].reshape(256, b - a)
        for e in range(2):
            GU[e, :, :, r] += dot(rows, WGU[e, h, a:b]).reshape(4, 4, 16, 512)

    def experts_y(yy):
        a, b = cols(2)
        for h in range(2):
            rows = X[:, yy, :, h, :, a:b].reshape(128, b - a)
            for e in range(2):
                GU[e, :, yy] += dot(rows, WGU[e, h, a:b]).reshape(4, 2, 16, 512)

    def experts(d):
        experts_z((z + d) % 4)
        experts_x((x + d) % 4)
        experts_y((y + d) % 4)

    experts(0)
    for ring in stages[2]:
        ring.forward()
    experts(1)
    experts(3)
    for ring in stages[2]:
        ring.finish()
    experts(2)

    wide = lax.broadcasted_iota(jnp.int32, (128, 128), 1) % 64

    def activate(zz):
        gates = X[zz, :, :, 0, :, HALF:].reshape(128, 128).astype(F32)
        for e in range(2):
            weight = jnp.sum(jnp.where(wide == p * 2 + e, gates, 0.0), axis=1, keepdims=True)
            gu = GU[e, zz].reshape(128, 512)
            act = jax.nn.silu(gu[:, :256]) * gu[:, 256:] * weight
            A[x, zz, :, :, e * 256 : e * 256 + 256] = act.astype(BF16).reshape(4, 32, 256)

    def act_ring(j):
        zz = (z + order[j]) % 4
        return Ring(
            13 + j, "x", lambda i: A.at[i, zz], lambda i: A.at[i, zz, pl.ds(0, 2)], lambda i: A.at[i, zz, pl.ds(2, 2)]
        )

    order = (2, 1, 3, 0)
    acts = [act_ring(j) for j in range(4)]
    over_y, over_z, last_z, last_y = [], [], [], []

    def down(j):
        zz = (z + order[j]) % 4
        for half, buf in ((1, Y1), (0, Y0)):
            acc = jnp.zeros((128, 896), F32)
            for i in range(4):
                acc += dot(A[i, zz].reshape(128, 512), WD[i, :, :, half * 896 : half * 896 + 896].reshape(512, 896))
            buf[j] = acc.reshape(4, 32, 896).astype(BF16)
            if half == 1 and j < 3:
                over_z.append(go(rcopy(Y1.at[j], R1.at[j], y1_s.at[j], y1_r.at[j], at(zz=zz))))
        group = []
        for m in range(3):
            yy = (y + order[m]) % 4
            group.append(go(rcopy(Y0.at[j, yy], R0.at[j, m], y0_s.at[j, m], y0_r.at[j, m], at(yy=yy))))
        over_y.append(group)

    def gather_y(j):
        zz = (z + order[j]) % 4
        for c in over_y[j]:
            c.wait_recv()
        acc = Y0[j, y].astype(F32)
        for m in range(3):
            acc += R0[j, m].astype(F32)
        if j < 3:
            T0[j] = acc.astype(BF16)
            last_z.append(go(rcopy(T0.at[j], Q0.at[j], y2_s.at[0, j], y2_r.at[0, j], at(zz=zz))))
        else:
            O0[...] = acc

    activate((z + order[0]) % 4)
    acts[0].start()
    activate((z + order[1]) % 4)
    acts[1].start()
    activate((z + order[2]) % 4)
    activate((z + order[3]) % 4)
    acts[0].forward()
    acts[2].start()
    for c in pass_on:
        c.wait_recv()
    acts[1].forward()
    acts[0].finish()
    acts[3].start()
    down(0)
    acts[2].forward()
    acts[1].finish()
    down(1)
    gather_y(0)
    acts[3].forward()
    acts[2].finish()
    down(2)
    gather_y(1)
    acts[3].finish()
    down(3)
    gather_y(2)
    for c in over_z:
        c.wait_recv()

    def sum_z(yy):
        acc = Y1[3, yy].astype(F32)
        for m in range(3):
            acc += R1[m, yy].astype(F32)
        return acc

    for m in range(3):
        yy = (y + order[m]) % 4
        T1[m] = sum_z(yy).astype(BF16)
        last_y.append(go(rcopy(T1.at[m], Q1.at[m], y2_s.at[1, m], y2_r.at[1, m], at(yy=yy))))
    gather_y(3)
    m0 = O0[...]
    m1 = sum_z(y)
    for c in to_out + last_z + last_y:
        c.wait_recv()
    for m in range(3):
        m0 += Q0[m].astype(F32)
        m1 += Q1[m].astype(F32)
    for r in range(2):
        rows = slice(r * 16, r * 16 + 16)
        low = jnp.concatenate([RL[r * 2 + h, i] for i in range(2) for h in range(2)], axis=1)
        high = jnp.concatenate([RL[r * 2 + h, i] for i in range(2, 4) for h in range(2)], axis=1)
        out_ref[rows, 0:896] = (low + m0[rows]).astype(BF16)
        out_ref[rows, 896:1792] = (high + m1[rows]).astype(BF16)

    for c in sends:
        c.wait_send()
    wgu_all.wait_send()


def body(
    hidden_in, queries, latent_cache, new_latent, cache_lengths, value_up, out_proj, norm_gain, router, expert_ids,
    w_gate_up, w_down,
):
    wgu = w_gate_up[0].reshape(7168, 2, 2, 128).transpose(0, 2, 1, 3).reshape(28672, 128)
    any_spec = pl.BlockSpec(memory_space=pl.ANY)
    vmem = pl.BlockSpec(memory_space=pltpu.VMEM)
    dma = pltpu.SemaphoreType.DMA
    return pl.pallas_call(
        layer_kernel,
        out_shape=jax.ShapeDtypeStruct((32, 1792), BF16),
        in_specs=[any_spec] * 6 + [vmem] * 5 + [pl.BlockSpec(memory_space=pltpu.SMEM)],
        out_specs=vmem,
        scratch_shapes=[
            pltpu.VMEM((2, GROUP, 208, 576), BF16),
            pltpu.VMEM((32, 32, 576), BF16),
            pltpu.VMEM((32, 576), F32),
            pltpu.VMEM((4, 1024, 128), F32),
            pltpu.VMEM((32, 512, 128), BF16),
            pltpu.VMEM((2, 3584, 128), BF16),
            pltpu.VMEM((256, 256), BF16),
            pltpu.VMEM((16, 16, 224), F32),
            pltpu.VMEM((1, HALF), F32),
            pltpu.VMEM((128, HALF), BF16),
            pltpu.VMEM((16, 128), F32),
            pltpu.VMEM((4, 4, 32, 4096), BF16),
            pltpu.VMEM((2, 224, 4096), BF16),
            pltpu.VMEM((2, 4, 4, 32, 224), F32),
            pltpu.VMEM((4, 4, 4, 16, 224), BF16),
            pltpu.VMEM((4, 4, 4, 16, 224), BF16),
            pltpu.VMEM((4, 4, 16, 224), BF16),
            pltpu.VMEM((16, 16, 224), BF16),
            pltpu.VMEM((16, 128), F32),
            pltpu.VMEM((16, 128), F32),
            pltpu.VMEM((16, 16, 224), F32),
            pltpu.VMEM((4, 4, 16, 224), F32),
            pltpu.VMEM((4, 4, 2, 2, 16, 3712), BF16),
            pltpu.VMEM((2, 2, HALF, 512), BF16),
            pltpu.VMEM((2, 4, 4, 2, 16, 512), F32),
            pltpu.VMEM((4, 2, 256, 1792), BF16),
            pltpu.VMEM((4, 4, 4, 32, 512), BF16),
            pltpu.VMEM((4, 4, 32, 896), BF16),
            pltpu.VMEM((4, 4, 32, 896), BF16),
            pltpu.VMEM((4, 3, 32, 896), BF16),
            pltpu.VMEM((3, 4, 32, 896), BF16),
            pltpu.VMEM((3, 32, 896), BF16),
            pltpu.VMEM((3, 32, 896), BF16),
            pltpu.VMEM((3, 32, 896), BF16),
            pltpu.VMEM((3, 32, 896), BF16),
            pltpu.VMEM((32, 896), F32),
            dma((17, 4)),
            dma((17, 4)),
            dma((3,)),
            dma((3,)),
            dma((15,)),
            dma((15,)),
            dma((1,)),
            dma((1,)),
            dma((3,)),
            dma((3,)),
            dma((1,)),
            dma((1,)),
            dma((1,)),
            dma((1,)),
            dma((3,)),
            dma((3,)),
            dma((4,)),
            dma((4,)),
            dma((4, 3)),
            dma((4, 3)),
            dma((3,)),
            dma((3,)),
            dma((2, 3)),
            dma((2, 3)),
            dma((4,)),
            dma((2,)),
            dma((2,)),
        ],
        compiler_params=pltpu.CompilerParams(
            collective_id=0, has_side_effects=True, vmem_limit_bytes=66_000_000
        ),
        name="layer",
    )(
        queries, latent_cache, value_up, out_proj.T, wgu, w_down[0], new_latent, hidden_in, norm_gain.reshape(1, -1),
        router.T, expert_ids.T, cache_lengths,
    )


def solution(mesh):
    in_specs = (
        P("batch", None),
        P("batch", ("sec", "head"), None),
        P("batch", None, None),
        P("batch", None),
        P("batch"),
        P(("sec", "head"), None, None),
        P(("sec", "head"), "batch"),
        P(),
        P(),
        P("batch", None),
        P("batch", None, None, ("sec", "head")),
        P("batch", ("sec", "head"), None),
    )
    out_specs = P("batch", ("sec", "head"))
    return jax.shard_map(body, mesh=mesh, in_specs=in_specs, out_specs=out_specs, check_vma=False)
```

time: 182 us -> 141 us (0.77)
  local copies, waits for them, and re-layouts: 22.3 us -> 1.55 us
  matrix products: 13.3 us -> 0 us
  other arithmetic: 3.88 us -> 0 us
  Pallas kernels: 142 us -> 140 us
    dot_general x4 -> x0, matrix products: 13.3 us -> none  [the longest x1 6.24 us: body(): jnp.einsum('thk,tjk->thj', queries, latent_cache, preferred_element_type=...]
    another operation x1 -> x0, local copies, waits for them, and re-layouts: 12.4 us -> none  [body(): wgu = w_gate_up[0].reshape(16, 2, 224, 512)]
    reshape x5 -> x0, local copies, waits for them, and re-layouts: 4 us -> none  [the longest x1 0.87 us: body(): norm_gain.reshape(16, 2, 224)]
    unnamed x14 -> x1, local copies, waits for them, and re-layouts: 4.65 us -> 1.55 us
    pallas_call x1, Pallas kernels: 142 us -> 140 us  [body(): pl.pallas_call(layer_kernel, out_shape=jax.ShapeDtypeStruct((32, 1792), B...]
    concatenate x1 -> x0, other arithmetic: 1.98 us -> none  [body(): rout = jnp.concatenate([rout, blank, rout, blank], axis=1)]
where the time goes in v2:
time: 141 us
  Pallas kernels  140 us (99%)
  local copies, waits for them, and re-layouts  1.55 us (1%)
    pallas_call x1, Pallas kernels, body(): pl.pallas_call(layer_kernel, out_shape=jax.ShapeDtypeStruct((32, 1792), B...  140 us

profile of v2, /device:TPU:0, one launch (start us, length us, event | category | flops | bytes accessed | tf_op | source)
XLA Modules:
  0.0 141.2 jit_solution(1491324221466098445)
XLA Ops:
  0.0 139.6 %layer.1 = bf16[32,1792]{1,0:T(8,128)(2,1)} custom-call(bf16[32,32,576]{2,1,0:T(8,128)(2,1)} %q_hbm.1, bf16[32,192,576]{2,1,0:T(8,128)(2,1)} %cache_hbm.1, bf16[32,512,128]{2,1,0:T(8,128)(2,1)} %vu_hbm.1, bf16[224,4096]{1,0:T(8,128)(2,1)} %bitcast.12, bf16[28672,128]{1,0:T(8,128)(2,1)} %bitcast.10, bf16[256,7168]{1,0:T(8,128)(2,1)} %bitcast.11, ...), custom_call_target="tpu_custom_call" | custom-call | tf_op jit(solution)/shard_map/layer/pallas_call | solution.py:530
  139.6 1.6 %copy.15 = bf16[32,1792]{1,0:T(8,128)(2,1)} copy(bf16[32,1792]{1,0:T(8,128)(2,1)} %layer.1) | data formatting | bytes 229376

commit v3 on v2

--- a/solution.py
+++ b/solution.py
@@ -175,25 +175,27 @@
             self.far_up.wait_recv()
             self.far_down.wait_recv()
 
-    def head_ring(k, dim, half, other_full):
+    def head_ring(k, dim, half, other):
         def view(rows):
             def part(i):
                 cols = pl.ds(half * 2048, 2048)
                 if dim == "z":
-                    return H.at[i, :, rows, cols] if other_full else H.at[i, y, rows, cols]
-                return H.at[:, i, rows, cols] if other_full else H.at[z, i, rows, cols]
+                    return H.at[i, (y + other) % 4, rows, cols]
+                return H.at[(z + other) % 4, i, rows, cols]
 
             return part
 
         return Ring(k, dim, view(pl.ds(0, 32)), view(pl.ds(0, 16)), view(pl.ds(16, 16)))
 
-    h0a, h0b = head_ring(0, "y", 0, False), head_ring(1, "z", 0, True)
-    h1a, h1b = head_ring(2, "z", 1, False), head_ring(3, "y", 1, True)
+    h0a, h0b = head_ring(0, "y", 0, 0), [head_ring(1 + o, "z", 0, o) for o in range(4)]
+    h1a, h1b = head_ring(5, "z", 1, 0), [head_ring(6 + o, "y", 1, o) for o in range(4)]
 
     lax.fori_loop(0, 16, head_values, 0)
     h0a.start()
+    h0b[0].start()
     lax.fori_loop(16, 32, head_values, 0)
     h1a.start()
+    h1b[0].start()
 
     spread_row = lax.broadcasted_iota(jnp.int32, (256, 256), 0)
     spread_col = lax.broadcasted_iota(jnp.int32, (256, 256), 1)
@@ -244,18 +246,28 @@
         HIT[...] = dot_t(jnp.where(mine, 1.0, 0.0).astype(BF16), hit.astype(BF16))
 
     ACC[...] = jnp.zeros_like(ACC)
-    lax.fori_loop(0, 2, separate, 0)
+    lax.fori_loop(0, 1, separate, 0)
     h0a.forward()
     h1a.forward()
+    for o in (1, 3):
+        h0b[o].start()
+        h1b[o].start()
+    lax.fori_loop(1, 2, separate, 0)
+    h0b[0].forward()
+    h1b[0].forward()
+    h0a.finish()
+    h0b[2].start()
+    h1a.finish()
+    h1b[2].start()
     lax.fori_loop(2, 4, separate, 0)
-    h0a.finish()
-    h0b.start()
-    h1a.finish()
-    h1b.start()
     for i in range(4):
         for h in range(2):
             far_wgu(i, h).start()
-    lax.fori_loop(4, 8, separate, 0)
+    lax.fori_loop(4, 7, separate, 0)
+    for o in (1, 3):
+        h0b[o].forward()
+        h1b[o].forward()
+    lax.fori_loop(7, 8, separate, 0)
     pack_inputs()
     for i in range(4, 8):
         for h in range(2):
@@ -279,12 +291,13 @@
         project_y((y + d) % 4)
 
     project(0)
-    h0b.forward()
-    h1b.forward()
+    h0b[2].forward()
+    h1b[2].forward()
     project(1)
     project(3)
-    h0b.finish()
-    h1b.finish()
+    for o in range(4):
+        h0b[o].finish()
+        h1b[o].finish()
     project(2)
 
     for r in range(2):
@@ -315,56 +328,70 @@
     square = jnp.sum(res * res, axis=1, keepdims=True)
     note = dot_t(scaled.astype(BF16), ROUT[...])
     MS[...] = jnp.where(lane == 32, square, note)
+    X[z, y, head, sec, :, 0:HALF] = scaled.astype(BF16)
     msg = go(rcopy(MS, MR, m_s.at[0], m_r.at[0], at(xx=x + 1 - 2 * sec)))
+    def row_ring(k, part, dim, done, fixed):
+        c0, c1, c2 = PARTS[part]
+
+        def view(a, b):
+            def block(i):
+                at_dim = {}
+                for d in "zyx":
+                    at_dim[d] = i if d == dim else None if d in done else (dims[d] + fixed.get(d, 0)) % 4
+                zi, yi, xi = (slice(None) if at_dim[d] is None else at_dim[d] for d in "zyx")
+                if at_dim["x"] is None:
+                    return X.at[zi, yi, :, :, :, pl.ds(a, b - a)]
+                return X.at[zi, yi, xi // 2, xi % 2, :, pl.ds(a, b - a)]
+
+            return block
+
+        return Ring(k, dim, view(c0, c2), view(c0, c1), view(c1, c2))
+
+    first, second, third = [], [], []
+    for part, (d1, d2, d3) in enumerate(("xyz", "yzx", "zxy")):
+        first.append(row_ring(10 + part, part, d1, "", {}))
+        second.append(row_ring(13 + part, part, d2, d1, {}))
+        third.append([row_ring(16 + part * 4 + o, part, d3, d1, {d2: o}) for o in range(4)])
+    GU[...] = jnp.zeros_like(GU)
+    first[0].start()
+    first[1].start()
+
+    msg.wait_recv()
+    both = MS[...] + MR[...]
+    mean_square = jnp.sum(jnp.where(lane == 32, both, 0.0), axis=1, keepdims=True) / (2 * HALF)
+    inv = lax.rsqrt(mean_square + norm_epsilon)
+    affinity = jax.nn.sigmoid(both * inv)
+    picked = jnp.where(HIT[...] > 0.0, affinity, 0.0)
+    gate = route_scale * picked / jnp.sum(picked, axis=1, keepdims=True)
+    gate = jnp.where(lane == 32, inv, gate)
+    top = gate.astype(BF16).astype(F32)
+    X[z, y, head, sec, :, HALF:] = (top + pltpu.roll(gate - top, 64, 1)).astype(BF16)
+    first[2].start()
+
+    for ring in first:
+        ring.forward()
+    for before, ring in zip(first, second):
+        before.finish()
+        ring.start()
+    for rings in third:
+        rings[0].start()
+    for ring in second:
+        ring.forward()
+    for rings in third:
+        rings[1].start()
+        rings[3].start()
+
     to_out = []
     for d in range(1, 4):
         xx = (x + d) % 4
         s = (xx % 2) * 2 + xx // 2
         to_out.append(go(rcopy(RF.at[pl.ds(s * 4, 4)], RL.at[x], rl_s.at[d - 1], rl_r.at[d - 1], at(xx=xx))))
     RL[x] = RF[pl.ds((sec * 2 + head) * 4, 4)]
-    msg.wait_recv()
-    both = MS[...] + MR[...]
-    mean_square = jnp.sum(jnp.where(lane == 32, both, 0.0), axis=1, keepdims=True) / (2 * HALF)
-    inv = lax.rsqrt(mean_square + norm_epsilon)
-    X[z, y, head, sec, :, 0:HALF] = (scaled * inv).astype(BF16)
-    affinity = jax.nn.sigmoid(both * inv)
-    picked = jnp.where(HIT[...] > 0.0, affinity, 0.0)
-    gate = route_scale * picked / jnp.sum(picked, axis=1, keepdims=True)
-    top = gate.astype(BF16).astype(F32)
-    X[z, y, head, sec, :, HALF:] = (top + pltpu.roll(gate - top, 64, 1)).astype(BF16)
-
-    def row_ring(k, part, dim, done):
-        c0, c1, c2 = PARTS[part]
-
-        def view(a, b):
-            def block(i):
-                zi = i if dim == "z" else slice(None) if "z" in done else z
-                yi = i if dim == "y" else slice(None) if "y" in done else y
-                if "x" in done:
-                    return X.at[zi, yi, :, :, :, pl.ds(a, b - a)]
-                xi = i if dim == "x" else x
-                return X.at[zi, yi, xi // 2, xi % 2, :, pl.ds(a, b - a)]
-
-            return block
-
-        return Ring(k, dim, view(c0, c2), view(c0, c1), view(c1, c2))
-
-    orders = ("xyz", "yzx", "zxy")
-    stages = [
-        [row_ring(4 + st * 3 + part, part, orders[part][st], orders[part][:st]) for part in range(3)] for st in range(3)
-    ]
-    GU[...] = jnp.zeros_like(GU)
-    for st in range(3):
-        if st > 0:
-            for ring, before in zip(stages[st], stages[st - 1]):
-                before.finish()
-                ring.start()
-        else:
-            for ring in stages[st]:
-                ring.start()
-        if st < 2:
-            for ring in stages[st]:
-                ring.forward()
+    for rings in third:
+        rings[0].forward()
+    for before, rings in zip(second, third):
+        before.finish()
+        rings[2].start()
 
     for c in send_wd:
         c.wait_recv()
@@ -405,28 +432,31 @@
         experts_y((y + d) % 4)
 
     experts(0)
-    for ring in stages[2]:
-        ring.forward()
+    for o in (1, 3, 2):
+        for rings in third:
+            rings[o].forward()
     experts(1)
     experts(3)
-    for ring in stages[2]:
-        ring.finish()
+    for o in range(4):
+        for rings in third:
+            rings[o].finish()
     experts(2)
 
     wide = lax.broadcasted_iota(jnp.int32, (128, 128), 1) % 64
 
     def activate(zz):
         gates = X[zz, :, :, 0, :, HALF:].reshape(128, 128).astype(F32)
+        inv = jnp.sum(jnp.where(wide == 32, gates, 0.0), axis=1, keepdims=True)
         for e in range(2):
             weight = jnp.sum(jnp.where(wide == p * 2 + e, gates, 0.0), axis=1, keepdims=True)
-            gu = GU[e, zz].reshape(128, 512)
+            gu = GU[e, zz].reshape(128, 512) * inv
             act = jax.nn.silu(gu[:, :256]) * gu[:, 256:] * weight
             A[x, zz, :, :, e * 256 : e * 256 + 256] = act.astype(BF16).reshape(4, 32, 256)
 
     def act_ring(j):
         zz = (z + order[j]) % 4
         return Ring(
-            13 + j, "x", lambda i: A.at[i, zz], lambda i: A.at[i, zz, pl.ds(0, 2)], lambda i: A.at[i, zz, pl.ds(2, 2)]
+            28 + j, "x", lambda i: A.at[i, zz], lambda i: A.at[i, zz, pl.ds(0, 2)], lambda i: A.at[i, zz, pl.ds(2, 2)]
         )
 
     order = (2, 1, 3, 0)
@@ -569,8 +599,8 @@
             pltpu.VMEM((3, 32, 896), BF16),
             pltpu.VMEM((3, 32, 896), BF16),
             pltpu.VMEM((32, 896), F32),
-            dma((17, 4)),
-            dma((17, 4)),
+            dma((32, 4)),
+            dma((32, 4)),
             dma((3,)),
             dma((3,)),
             dma((15,)),

time: 141 us -> 137 us (0.972)
  Pallas kernels: 140 us -> 136 us
    pallas_call x1, Pallas kernels: 140 us -> 136 us  [body(): pl.pallas_call(layer_kernel, out_shape=jax.ShapeDtypeStruct((32, 1792), B...]
where the time goes in v3:
time: 137 us
  Pallas kernels  136 us (99%)
  local copies, waits for them, and re-layouts  1.55 us (1%)
    pallas_call x1, Pallas kernels, body(): pl.pallas_call(layer_kernel, out_shape=jax.ShapeDtypeStruct((32, 1792), B...  136 us

profile of v3, /device:TPU:0, one launch (start us, length us, event | category | flops | bytes accessed | tf_op | source)
XLA Modules:
  0.0 137.1 jit_solution(2573561800093643210)
XLA Ops:
  0.0 135.5 %layer.1 = bf16[32,1792]{1,0:T(8,128)(2,1)} custom-call(bf16[32,32,576]{2,1,0:T(8,128)(2,1)} %q_hbm.1, bf16[32,192,576]{2,1,0:T(8,128)(2,1)} %cache_hbm.1, bf16[32,512,128]{2,1,0:T(8,128)(2,1)} %vu_hbm.1, bf16[224,4096]{1,0:T(8,128)(2,1)} %bitcast.12, bf16[28672,128]{1,0:T(8,128)(2,1)} %bitcast.10, bf16[256,7168]{1,0:T(8,128)(2,1)} %bitcast.11, ...), custom_call_target="tpu_custom_call" | custom-call | tf_op jit(solution)/shard_map/layer/pallas_call | solution.py:560
  135.6 1.6 %copy.15 = bf16[32,1792]{1,0:T(8,128)(2,1)} copy(bf16[32,1792]{1,0:T(8,128)(2,1)} %layer.1) | data formatting | bytes 229376

commit v4 on v3

--- a/solution.py
+++ b/solution.py
@@ -12,7 +12,7 @@
 
 BF16, F32 = jnp.bfloat16, jnp.float32
 MESH = pl.DeviceIdType.MESH
-PARTS = ((0, 640, 1280), (1280, 1920, 2560), (2560, 3200, 3712))
+PARTS = ((0, 768, 1408), (1408, 1920, 2304), (2304, 3072, 3712))
 HALF = 3584
 GROUP = 8
 
@@ -93,15 +93,11 @@
     own_vu.start()
     own_wo = lcopy(wo_hbm, WO.at[core], 1)
     own_wo.start()
-    raw_copy(0, 0).start()
-    raw_copy(1, 1).start()
 
     def wd_cols(xx):
         s = (xx % 2) * 2 + xx // 2
         return wd_hbm.at[:, pl.ds(pl.multiple_of(s * 1792, 128), 1792)]
 
-    own_wd = lcopy(wd_cols(x), WD.at[x, core], 3)
-    own_wd.start()
     NEW[...] = new_ref[...].astype(F32)
     own_q.wait()
     pl.semaphore_wait(barrier, 19)
@@ -109,9 +105,16 @@
     other_core = at(cc=1 - core)
     send_wo = go(rcopy(wo_hbm, WO.at[core], wo_s.at[0], wo_r.at[0], other_core))
     send_wd = []
-    for d in (1, 3, 2):
+    for d in (1, 3):
         xx = (x + d) % 4
         send_wd.append(go(rcopy(wd_cols(xx), WD.at[x, core], wd_s.at[d - 1], wd_r.at[d - 1], at(xx=xx))))
+    opposite = (x + 2) % 4
+
+    def far_wd(k, rows):
+        src, dst = wd_cols(opposite).at[rows], WD.at[x, core, rows]
+        send_wd.append(go(rcopy(src, dst, wd_s.at[k], wd_r.at[k], at(xx=opposite))))
+
+    far_wd(1, pl.ds(0, 128))
 
     own_row = lax.broadcasted_iota(jnp.int32, (16, 576), 0) == 0
     column = lax.broadcasted_iota(jnp.int32, (GROUP * 32, 208), 1)
@@ -140,11 +143,17 @@
         return carry
 
     lax.fori_loop(0, 32 // GROUP, attend, 0)
+    raw_copy(0, 0).start()
+    raw_copy(1, 1).start()
+    own_wd = lcopy(wd_cols(x), WD.at[x, core], 3)
+    own_wd.start()
     own_vu.wait()
 
-    def head_values(h, carry):
-        latent = jnp.concatenate([L[c, pl.ds(h, 32, stride=32), :] for c in range(4)], axis=1).astype(BF16)
-        H[z, y, :, pl.ds(pl.multiple_of(h * 128, 128), 128)] = dot(latent, VU[h]).astype(BF16)
+    def head_values(i, carry):
+        for j in range(4):
+            h = i * 4 + j
+            latent = jnp.concatenate([L[c, pl.ds(h, 32, stride=32), :] for c in range(4)], axis=1).astype(BF16)
+            H[z, y, :, pl.ds(pl.multiple_of(h * 128, 128), 128)] = dot(latent, VU[h]).astype(BF16)
         return carry
 
     dims = {"z": z, "y": y, "x": x}
@@ -190,10 +199,10 @@
     h0a, h0b = head_ring(0, "y", 0, 0), [head_ring(1 + o, "z", 0, o) for o in range(4)]
     h1a, h1b = head_ring(5, "z", 1, 0), [head_ring(6 + o, "y", 1, o) for o in range(4)]
 
-    lax.fori_loop(0, 16, head_values, 0)
+    lax.fori_loop(0, 4, head_values, 0)
     h0a.start()
     h0b[0].start()
-    lax.fori_loop(16, 32, head_values, 0)
+    lax.fori_loop(4, 8, head_values, 0)
     h1a.start()
     h1b[0].start()
 
@@ -307,6 +316,7 @@
     for d in (2, 1, 3):
         xx = (x + d) % 4
         cross.append(go(rcopy(PS.at[xx], RX.at[x], bx_s.at[d - 1], bx_r.at[d - 1], at(xx=xx))))
+    far_wd(3, pl.ds(128, 128))
     for c in cross:
         c.wait_recv()
     total = PS[x].astype(F32)
@@ -613,8 +623,8 @@
             dma((1,)),
             dma((1,)),
             dma((1,)),
-            dma((3,)),
-            dma((3,)),
+            dma((4,)),
+            dma((4,)),
             dma((4,)),
             dma((4,)),
             dma((4, 3)),

time: 137 us -> 132 us (0.964)
  Pallas kernels: 136 us -> 130 us
    pallas_call x1, Pallas kernels: 136 us -> 130 us  [body(): pl.pallas_call(layer_kernel, out_shape=jax.ShapeDtypeStruct((32, 1792), B...]
where the time goes in v4:
time: 132 us; the launch traced here: 131 us
  Pallas kernels  130 us (98%)
  local copies, waits for them, and re-layouts  1.55 us (1%)
    pallas_call x1, Pallas kernels, body(): pl.pallas_call(layer_kernel, out_shape=jax.ShapeDtypeStruct((32, 1792), B...  130 us

profile of v4, /device:TPU:0, one launch (start us, length us, event | category | flops | bytes accessed | tf_op | source)
XLA Modules:
  0.0 131.3 jit_solution(6862545838523371041)
XLA Ops:
  0.0 129.8 %layer.1 = bf16[32,1792]{1,0:T(8,128)(2,1)} custom-call(bf16[32,32,576]{2,1,0:T(8,128)(2,1)} %q_hbm.1, bf16[32,192,576]{2,1,0:T(8,128)(2,1)} %cache_hbm.1, bf16[32,512,128]{2,1,0:T(8,128)(2,1)} %vu_hbm.1, bf16[224,4096]{1,0:T(8,128)(2,1)} %bitcast.12, bf16[28672,128]{1,0:T(8,128)(2,1)} %bitcast.10, bf16[256,7168]{1,0:T(8,128)(2,1)} %bitcast.11, ...), custom_call_target="tpu_custom_call" | custom-call | tf_op jit(solution)/shard_map/layer/pallas_call | solution.py:570
  129.8 1.6 %copy.15 = bf16[32,1792]{1,0:T(8,128)(2,1)} copy(bf16[32,1792]{1,0:T(8,128)(2,1)} %layer.1) | data formatting | bytes 229376

commit v5 on v4

--- a/solution.py
+++ b/solution.py
@@ -29,8 +29,8 @@
     q_hbm, cache_hbm, vu_hbm, wo_hbm, wgu_hbm, wd_hbm, new_ref, hidden_ref, gain_ref, router_ref, ids_ref, len_ref,
     out_ref,
     CA, Q, NEW, L, VU, RAW, PERM, HID, GAIN, ROUT, HIT,
-    H, WO, ACC, PS, RX, SS, RY, MS, MR, RF, RL, X, WGU, GU, WD, A, Y0, Y1, R0, R1, T0, T1, Q0, Q1, O0,
-    ring_s, ring_r, bx_s, bx_r, by_s, by_r, m_s, m_r, rl_s, rl_r, wo_s, wo_r, wg_s, wg_r, wd_s, wd_r, wf_s, wf_r,
+    H, WO, ACC, PS, RX, MS, MR, RF, RL, X, WGU, GU, WD, A, Y0, Y1, R0, R1, T0, T1, Q0, Q1, O0,
+    ring_s, ring_r, by_s, by_r, m_s, m_r, rl_s, rl_r, wo_s, wo_r, wg_s, wg_r, wd_s, wd_r, wf_s, wf_r,
     y0_s, y0_r, y1_s, y1_r, y2_s, y2_r, loc, ca_sem, raw_sem,
 ):
     sec = lax.axis_index("sec")
@@ -55,11 +55,16 @@
         pl.semaphore_signal(barrier, inc=1, device_id=to, device_id_type=MESH)
 
     greet(at(cc=1 - core))
-    for d in range(1, 4):
-        greet(at(xx=(x + d) % 4))
-    for d in range(1, 16):
-        q = (p + d) % 16
-        greet(at(zz=q // 4, yy=q % 4))
+
+    def offset(i):
+        return (z + i // 16) % 4, (y + i // 4 % 4) % 4, (x + i % 4) % 4
+
+    def greet_step(i, carry):
+        zz, yy, xx = offset(i)
+        greet(at(zz=zz, yy=yy, xx=xx))
+        return carry
+
+    lax.fori_loop(1, 64, greet_step, 0)
 
     def rcopy(src, dst, send, recv, to):
         return pltpu.make_async_remote_copy(
@@ -100,7 +105,7 @@
 
     NEW[...] = new_ref[...].astype(F32)
     own_q.wait()
-    pl.semaphore_wait(barrier, 19)
+    pl.semaphore_wait(barrier, 64)
 
     other_core = at(cc=1 - core)
     send_wo = go(rcopy(wo_hbm, WO.at[core], wo_s.at[0], wo_r.at[0], other_core))
@@ -312,26 +317,32 @@
     for r in range(2):
         for h in range(2):
             PS[r * 2 + h] = ACC[h, :, :, r * 16 : r * 16 + 16, :].astype(BF16)
-    cross = []
-    for d in (2, 1, 3):
-        xx = (x + d) % 4
-        cross.append(go(rcopy(PS.at[xx], RX.at[x], bx_s.at[d - 1], bx_r.at[d - 1], at(xx=xx))))
+
+    def partial_copy(i):
+        zz, yy, xx = offset(i)
+        return rcopy(PS.at[xx, zz, yy], RX.at[x, p], by_s.at[i - 1], by_r.at[i - 1], at(zz=zz, yy=yy, xx=xx))
+
+    def partial_start(i, carry):
+        partial_copy(64 - i).start()
+        return carry
+
+    def partial_arrived(i, carry):
+        partial_copy(64 - i).wait_recv()
+        return carry
+
+    def partial_sent(i, carry):
+        partial_copy(i).wait_send()
+        return carry
+
+    lax.fori_loop(1, 64, partial_start, 0)
     far_wd(3, pl.ds(128, 128))
-    for c in cross:
-        c.wait_recv()
-    total = PS[x].astype(F32)
-    for d in range(1, 4):
-        total += RX[(x + d) % 4].astype(F32)
-    SS[...] = total.astype(BF16)
-    plane = []
-    for d in range(1, 16):
-        q = (p + d) % 16
-        plane.append(go(rcopy(SS.at[q // 4, q % 4], RY.at[p], by_s.at[d - 1], by_r.at[d - 1], at(zz=q // 4, yy=q % 4))))
-    RY[p] = SS[z, y]
-    for c in plane:
-        c.wait_recv()
-
-    RF[...] = RY[...].astype(F32) + HID[...]
+    RX[x, p] = PS[x, z, y]
+    lax.fori_loop(1, 64, partial_arrived, 0)
+
+    total = HID[...]
+    for i in range(4):
+        total += RX[i].astype(F32)
+    RF[...] = total
     res = jnp.concatenate([RF[i] for i in range(16)], axis=1)
     scaled = res * GAIN[...]
     lane = lax.broadcasted_iota(jnp.int32, (16, 128), 1)
@@ -557,6 +568,7 @@
     for c in sends:
         c.wait_send()
     wgu_all.wait_send()
+    lax.fori_loop(1, 64, partial_sent, 0)
 
 
 def body(
@@ -588,9 +600,7 @@
             pltpu.VMEM((2, 224, 4096), BF16),
             pltpu.VMEM((2, 4, 4, 32, 224), F32),
             pltpu.VMEM((4, 4, 4, 16, 224), BF16),
-            pltpu.VMEM((4, 4, 4, 16, 224), BF16),
-            pltpu.VMEM((4, 4, 16, 224), BF16),
-            pltpu.VMEM((16, 16, 224), BF16),
+            pltpu.VMEM((4, 16, 16, 224), BF16),
             pltpu.VMEM((16, 128), F32),
             pltpu.VMEM((16, 128), F32),
             pltpu.VMEM((16, 16, 224), F32),
@@ -611,10 +621,8 @@
             pltpu.VMEM((32, 896), F32),
             dma((32, 4)),
             dma((32, 4)),
-            dma((3,)),
-            dma((3,)),
-            dma((15,)),
-            dma((15,)),
+            dma((63,)),
+            dma((63,)),
             dma((1,)),
             dma((1,)),
             dma((3,)),

time: 132 us -> 134 us (1.015)
  Pallas kernels: 130 us -> 132 us
    pallas_call x1, Pallas kernels: 130 us -> 132 us  [body(): pl.pallas_call(layer_kernel, out_shape=jax.ShapeDtypeStruct((32, 1792), B...]
where the time goes in v5:
time: 134 us
  Pallas kernels  132 us (99%)
  local copies, waits for them, and re-layouts  1.55 us (1%)
    pallas_call x1, Pallas kernels, body(): pl.pallas_call(layer_kernel, out_shape=jax.ShapeDtypeStruct((32, 1792), B...  132 us

profile of v5, /device:TPU:0, one launch (start us, length us, event | category | flops | bytes accessed | tf_op | source)
XLA Modules:
  0.0 133.6 jit_solution(16040495319107011515)
XLA Ops:
  0.0 132.0 %layer.1 = bf16[32,1792]{1,0:T(8,128)(2,1)} custom-call(bf16[32,32,576]{2,1,0:T(8,128)(2,1)} %q_hbm.1, bf16[32,192,576]{2,1,0:T(8,128)(2,1)} %cache_hbm.1, bf16[32,512,128]{2,1,0:T(8,128)(2,1)} %vu_hbm.1, bf16[224,4096]{1,0:T(8,128)(2,1)} %bitcast.12, bf16[28672,128]{1,0:T(8,128)(2,1)} %bitcast.10, bf16[256,7168]{1,0:T(8,128)(2,1)} %bitcast.11, ...), custom_call_target="tpu_custom_call" | custom-call | tf_op jit(solution)/shard_map/layer/pallas_call | solution.py:582
  132.0 1.6 %copy.15 = bf16[32,1792]{1,0:T(8,128)(2,1)} copy(bf16[32,1792]{1,0:T(8,128)(2,1)} %layer.1) | data formatting | bytes 229376

commit v6 on v4

--- a/solution.py
+++ b/solution.py
@@ -142,19 +142,25 @@
 
         return carry
 
-    lax.fori_loop(0, 32 // GROUP, attend, 0)
+    lax.fori_loop(0, 16 // GROUP, attend, 0)
     raw_copy(0, 0).start()
     raw_copy(1, 1).start()
     own_wd = lcopy(wd_cols(x), WD.at[x, core], 3)
     own_wd.start()
     own_vu.wait()
 
-    def head_values(i, carry):
-        for j in range(4):
-            h = i * 4 + j
-            latent = jnp.concatenate([L[c, pl.ds(h, 32, stride=32), :] for c in range(4)], axis=1).astype(BF16)
-            H[z, y, :, pl.ds(pl.multiple_of(h * 128, 128), 128)] = dot(latent, VU[h]).astype(BF16)
-        return carry
+    def head_values(half):
+        rows = pl.ds(half * 16, 16)
+
+        def step(i, carry):
+            for j in range(4):
+                h = i * 4 + j
+                parts = [L[c, pl.ds(half * 512 + h, 16, stride=32), :] for c in range(4)]
+                latent = jnp.concatenate(parts, axis=1).astype(BF16)
+                H[z, y, rows, pl.ds(pl.multiple_of(h * 128, 128), 128)] = dot(latent, VU[h]).astype(BF16)
+            return carry
+
+        return step
 
     dims = {"z": z, "y": y, "x": x}
 
@@ -184,27 +190,60 @@
             self.far_up.wait_recv()
             self.far_down.wait_recv()
 
-    def head_ring(k, dim, half, other):
-        def view(rows):
+    def head_ring(k, dim, half, other, low):
+        def view(first, count):
             def part(i):
-                cols = pl.ds(half * 2048, 2048)
+                cols = pl.ds(half * 2048 + first, count)
+                rows = pl.ds(low * 16, 16)
                 if dim == "z":
                     return H.at[i, (y + other) % 4, rows, cols]
                 return H.at[(z + other) % 4, i, rows, cols]
 
             return part
 
-        return Ring(k, dim, view(pl.ds(0, 32)), view(pl.ds(0, 16)), view(pl.ds(16, 16)))
-
-    h0a, h0b = head_ring(0, "y", 0, 0), [head_ring(1 + o, "z", 0, o) for o in range(4)]
-    h1a, h1b = head_ring(5, "z", 1, 0), [head_ring(6 + o, "y", 1, o) for o in range(4)]
-
-    lax.fori_loop(0, 4, head_values, 0)
-    h0a.start()
-    h0b[0].start()
-    lax.fori_loop(4, 8, head_values, 0)
-    h1a.start()
-    h1b[0].start()
+        return Ring(k, dim, view(0, 2048), view(0, 1024), view(1024, 1024))
+
+    near, wide_rings = [], []
+    for low in range(2):
+        k = low * 10
+        near.append((head_ring(k, "y", 0, 0, low), head_ring(k + 1, "z", 1, 0, low)))
+        wide_rings.append(
+            [(head_ring(k + 2 + o, "z", 0, o, low), head_ring(k + 6 + o, "y", 1, o, low)) for o in range(4)]
+        )
+
+    def start_rows(low, half):
+        near[low][half].start()
+        wide_rings[low][0][half].start()
+
+    def near_forward(low):
+        for half in range(2):
+            near[low][half].forward()
+        for o in (1, 3):
+            for half in range(2):
+                wide_rings[low][o][half].start()
+
+    def near_finish(low):
+        for half in range(2):
+            wide_rings[low][0][half].forward()
+        for half in range(2):
+            near[low][half].finish()
+            wide_rings[low][2][half].start()
+
+    def wide_forward(low, o):
+        for half in range(2):
+            wide_rings[low][o][half].forward()
+
+    lax.fori_loop(0, 4, head_values(0), 0)
+    start_rows(0, 0)
+    lax.fori_loop(4, 8, head_values(0), 0)
+    start_rows(0, 1)
+    lax.fori_loop(16 // GROUP, 32 // GROUP, attend, 0)
+    near_forward(0)
+    lax.fori_loop(0, 4, head_values(1), 0)
+    start_rows(1, 0)
+    lax.fori_loop(4, 8, head_values(1), 0)
+    start_rows(1, 1)
+    near_finish(0)
 
     spread_row = lax.broadcasted_iota(jnp.int32, (256, 256), 0)
     spread_col = lax.broadcasted_iota(jnp.int32, (256, 256), 1)
@@ -256,26 +295,19 @@
 
     ACC[...] = jnp.zeros_like(ACC)
     lax.fori_loop(0, 1, separate, 0)
-    h0a.forward()
-    h1a.forward()
-    for o in (1, 3):
-        h0b[o].start()
-        h1b[o].start()
+    near_forward(1)
     lax.fori_loop(1, 2, separate, 0)
-    h0b[0].forward()
-    h1b[0].forward()
-    h0a.finish()
-    h0b[2].start()
-    h1a.finish()
-    h1b[2].start()
+    wide_forward(0, 1)
+    wide_forward(0, 3)
+    near_finish(1)
     lax.fori_loop(2, 4, separate, 0)
+    wide_forward(0, 2)
     for i in range(4):
         for h in range(2):
             far_wgu(i, h).start()
     lax.fori_loop(4, 7, separate, 0)
-    for o in (1, 3):
-        h0b[o].forward()
-        h1b[o].forward()
+    wide_forward(1, 1)
+    wide_forward(1, 3)
     lax.fori_loop(7, 8, separate, 0)
     pack_inputs()
     for i in range(4, 8):
@@ -300,13 +332,13 @@
         project_y((y + d) % 4)
 
     project(0)
-    h0b[2].forward()
-    h1b[2].forward()
+    wide_forward(1, 2)
     project(1)
     project(3)
-    for o in range(4):
-        h0b[o].finish()
-        h1b[o].finish()
+    for low in range(2):
+        for o in range(4):
+            for half in range(2):
+                wide_rings[low][o][half].finish()
     project(2)
 
     for r in range(2):
@@ -359,9 +391,9 @@
 
     first, second, third = [], [], []
     for part, (d1, d2, d3) in enumerate(("xyz", "yzx", "zxy")):
-        first.append(row_ring(10 + part, part, d1, "", {}))
-        second.append(row_ring(13 + part, part, d2, d1, {}))
-        third.append([row_ring(16 + part * 4 + o, part, d3, d1, {d2: o}) for o in range(4)])
+        first.append(row_ring(20 + part, part, d1, "", {}))
+        second.append(row_ring(23 + part, part, d2, d1, {}))
+        third.append([row_ring(26 + part * 4 + o, part, d3, d1, {d2: o}) for o in range(4)])
     GU[...] = jnp.zeros_like(GU)
     first[0].start()
     first[1].start()
@@ -466,7 +498,7 @@
     def act_ring(j):
         zz = (z + order[j]) % 4
         return Ring(
-            28 + j, "x", lambda i: A.at[i, zz], lambda i: A.at[i, zz, pl.ds(0, 2)], lambda i: A.at[i, zz, pl.ds(2, 2)]
+            38 + j, "x", lambda i: A.at[i, zz], lambda i: A.at[i, zz, pl.ds(0, 2)], lambda i: A.at[i, zz, pl.ds(2, 2)]
         )
 
     order = (2, 1, 3, 0)
@@ -609,8 +641,8 @@
             pltpu.VMEM((3, 32, 896), BF16),
             pltpu.VMEM((3, 32, 896), BF16),
             pltpu.VMEM((32, 896), F32),
-            dma((32, 4)),
-            dma((32, 4)),
+            dma((42, 4)),
+            dma((42, 4)),
             dma((3,)),
             dma((3,)),
             dma((15,)),

time: 132 us -> 132 us (level)
  no operation moved by 1% of the time
where the time goes in v6:
time: 132 us
  Pallas kernels  131 us (99%)
  local copies, waits for them, and re-layouts  1.55 us (1%)
    pallas_call x1, Pallas kernels, body(): pl.pallas_call(layer_kernel, out_shape=jax.ShapeDtypeStruct((32, 1792), B...  131 us

profile of v6, /device:TPU:0, one launch (start us, length us, event | category | flops | bytes accessed | tf_op | source)
XLA Modules:
  0.0 132.2 jit_solution(12149338056653435506)
XLA Ops:
  0.0 130.7 %layer.1 = bf16[32,1792]{1,0:T(8,128)(2,1)} custom-call(bf16[32,32,576]{2,1,0:T(8,128)(2,1)} %q_hbm.1, bf16[32,192,576]{2,1,0:T(8,128)(2,1)} %cache_hbm.1, bf16[32,512,128]{2,1,0:T(8,128)(2,1)} %vu_hbm.1, bf16[224,4096]{1,0:T(8,128)(2,1)} %bitcast.12, bf16[28672,128]{1,0:T(8,128)(2,1)} %bitcast.10, bf16[256,7168]{1,0:T(8,128)(2,1)} %bitcast.11, ...), custom_call_target="tpu_custom_call" | custom-call | tf_op jit(solution)/shard_map/layer/pallas_call | solution.py:602
  130.7 1.6 %copy.15 = bf16[32,1792]{1,0:T(8,128)(2,1)} copy(bf16[32,1792]{1,0:T(8,128)(2,1)} %layer.1) | data formatting | bytes 229376

commit v7 on v4

--- a/solution.py
+++ b/solution.py
@@ -316,7 +316,7 @@
     for d in (2, 1, 3):
         xx = (x + d) % 4
         cross.append(go(rcopy(PS.at[xx], RX.at[x], bx_s.at[d - 1], bx_r.at[d - 1], at(xx=xx))))
-    far_wd(3, pl.ds(128, 128))
+    far_wd(3, pl.ds(128, 64))
     for c in cross:
         c.wait_recv()
     total = PS[x].astype(F32)
@@ -357,14 +357,22 @@
 
         return Ring(k, dim, view(c0, c2), view(c0, c1), view(c1, c2))
 
-    first, second, third = [], [], []
+    first, second, third, third_own = [], [], [], []
     for part, (d1, d2, d3) in enumerate(("xyz", "yzx", "zxy")):
-        first.append(row_ring(10 + part, part, d1, "", {}))
-        second.append(row_ring(13 + part, part, d2, d1, {}))
-        third.append([row_ring(16 + part * 4 + o, part, d3, d1, {d2: o}) for o in range(4)])
+        k = 10 + part * 12
+        first.append(row_ring(k, part, d1, "", {}))
+        second.append([row_ring(k + 1 + o, part, d2, "", {d1: o}) for o in range(4)])
+        third_own.append([row_ring(k + 5 + o, part, d3, "", {d1: o}) for o in range(4)])
+        third.append([None] + [row_ring(k + 8 + o, part, d3, d1, {d2: o}) for o in range(1, 4)])
+
+    def start_part(part):
+        first[part].start()
+        second[part][0].start()
+        third_own[part][0].start()
+
     GU[...] = jnp.zeros_like(GU)
-    first[0].start()
-    first[1].start()
+    start_part(0)
+    start_part(1)
 
     msg.wait_recv()
     both = MS[...] + MR[...]
@@ -376,20 +384,26 @@
     gate = jnp.where(lane == 32, inv, gate)
     top = gate.astype(BF16).astype(F32)
     X[z, y, head, sec, :, HALF:] = (top + pltpu.roll(gate - top, 64, 1)).astype(BF16)
-    first[2].start()
-
-    for ring in first:
-        ring.forward()
-    for before, ring in zip(first, second):
-        before.finish()
-        ring.start()
-    for rings in third:
-        rings[0].start()
-    for ring in second:
-        ring.forward()
-    for rings in third:
-        rings[1].start()
-        rings[3].start()
+    start_part(2)
+    for part in range(3):
+        first[part].forward()
+        for o in (1, 3):
+            second[part][o].start()
+    for part in range(3):
+        second[part][0].forward()
+        for o in (1, 3):
+            third_own[part][o].start()
+    for part in range(3):
+        first[part].finish()
+        second[part][2].start()
+        third_own[part][2].start()
+    for part in range(3):
+        for o in (1, 3, 2):
+            second[part][o].forward()
+    for part in range(3):
+        third[part][1].start()
+        third[part][3].start()
+    far_wd(4, pl.ds(192, 64))
 
     to_out = []
     for d in range(1, 4):
@@ -397,10 +411,12 @@
         s = (xx % 2) * 2 + xx // 2
         to_out.append(go(rcopy(RF.at[pl.ds(s * 4, 4)], RL.at[x], rl_s.at[d - 1], rl_r.at[d - 1], at(xx=xx))))
     RL[x] = RF[pl.ds((sec * 2 + head) * 4, 4)]
-    for rings in third:
-        rings[0].forward()
+    for rings in third_own:
+        for o in (0, 1, 3, 2):
+            rings[o].forward()
     for before, rings in zip(second, third):
-        before.finish()
+        for o in range(4):
+            before[o].finish()
         rings[2].start()
 
     for c in send_wd:
@@ -448,6 +464,9 @@
     experts(1)
     experts(3)
     for o in range(4):
+        for rings in third_own:
+            rings[o].finish()
+    for o in range(1, 4):
         for rings in third:
             rings[o].finish()
     experts(2)
@@ -466,7 +485,7 @@
     def act_ring(j):
         zz = (z + order[j]) % 4
         return Ring(
-            28 + j, "x", lambda i: A.at[i, zz], lambda i: A.at[i, zz, pl.ds(0, 2)], lambda i: A.at[i, zz, pl.ds(2, 2)]
+            46 + j, "x", lambda i: A.at[i, zz], lambda i: A.at[i, zz, pl.ds(0, 2)], lambda i: A.at[i, zz, pl.ds(2, 2)]
         )
 
     order = (2, 1, 3, 0)
@@ -609,8 +628,8 @@
             pltpu.VMEM((3, 32, 896), BF16),
             pltpu.VMEM((3, 32, 896), BF16),
             pltpu.VMEM((32, 896), F32),
-            dma((32, 4)),
-            dma((32, 4)),
+            dma((50, 4)),
+            dma((50, 4)),
             dma((3,)),
             dma((3,)),
             dma((15,)),
@@ -623,8 +642,8 @@
             dma((1,)),
             dma((1,)),
             dma((1,)),
-            dma((4,)),
-            dma((4,)),
+            dma((5,)),
+            dma((5,)),
             dma((4,)),
             dma((4,)),
             dma((4, 3)),

time: 132 us -> 132 us (level)
  no operation moved by 1% of the time
where the time goes in v7:
time: 132 us
  Pallas kernels  131 us (99%)
  local copies, waits for them, and re-layouts  1.55 us (1%)
    pallas_call x1, Pallas kernels, body(): pl.pallas_call(layer_kernel, out_shape=jax.ShapeDtypeStruct((32, 1792), B...  131 us

profile of v7, /device:TPU:0, one launch (start us, length us, event | category | flops | bytes accessed | tf_op | source)
XLA Modules:
  0.0 132.2 jit_solution(13356020313406378232)
XLA Ops:
  0.0 130.6 %layer.1 = bf16[32,1792]{1,0:T(8,128)(2,1)} custom-call(bf16[32,32,576]{2,1,0:T(8,128)(2,1)} %q_hbm.1, bf16[32,192,576]{2,1,0:T(8,128)(2,1)} %cache_hbm.1, bf16[32,512,128]{2,1,0:T(8,128)(2,1)} %vu_hbm.1, bf16[224,4096]{1,0:T(8,128)(2,1)} %bitcast.12, bf16[28672,128]{1,0:T(8,128)(2,1)} %bitcast.10, bf16[256,7168]{1,0:T(8,128)(2,1)} %bitcast.11, ...), custom_call_target="tpu_custom_call" | custom-call | tf_op jit(solution)/shard_map/layer/pallas_call | solution.py:589
  130.6 1.6 %copy.15 = bf16[32,1792]{1,0:T(8,128)(2,1)} copy(bf16[32,1792]{1,0:T(8,128)(2,1)} %layer.1) | data formatting | bytes 229376
